TPU v7x, 512 devices: a whole 4x8x8 slice. The times are simulated.
512 devices in a mesh: req: 8 (over z), hid: 64 (over y, x, core).
Axes of the slice: x: 4, y: 8, z: 8, core: 2. Of those that a mesh axis runs over, the one named last changes fastest.
Arguments:
- residual_input: bfloat16 [4096, 2048], P('req', 'hid'), may hold values from -6 to 6
- queries: bfloat16 [4096, 2048], P('req'), may hold values from -31 to 31
- key_value_pairs: bfloat16 [4096, 1024], P('req'), may hold values from -4 to 4
- prompt_length_list: int32 [8, 6], P('req'), may hold values from 1 to 320, 512 in all within a row
- prompt_adapter_index: int32 [8, 6], P('req'), may hold values from 0 to 63
- adapter_position: int32 [64], replicated, may hold values from 0 to 63, each once
- output_matrix: bfloat16 [2048, 2048], P('req', 'hid'), may hold values from -0.125 to 0.125
- output_factor_first: bfloat16 [64, 2048, 16], P('hid'), may hold values from -0.125 to 0.125
- output_factor_second: bfloat16 [64, 16, 2048], P(None, None, 'hid'), may hold values from -1.5 to 1.5
- norm_weight: bfloat16 [2048], P('hid'), may hold values from 0.3984375 to 1.59375
- gate_up_matrix: bfloat16 [2048, 2, 8192], P('req', None, 'hid'), may hold values from -0.125 to 0.125
- gate_up_factor_first: bfloat16 [64, 2048, 32], P('hid'), may hold values from -0.125 to 0.125
- gate_up_factor_second: bfloat16 [2, 64, 16, 8192], P(None, None, None, 'hid'), may hold values from -1.5 to 1.5
- down_matrix: bfloat16 [8192, 2048], P('hid', 'req'), may hold values from -0.1875 to 0.1875
- down_factor_first: bfloat16 [8192, 64, 16], P('hid'), may hold values from -0.0625 to 0.0625
- down_factor_second: bfloat16 [64, 16, 2048], P(None, None, 'hid'), may hold values from -1.5 to 1.5
Outputs:
- stream_out: bfloat16 [4096, 2048], P('req', 'hid')
Inputs may be any that keep to these rules, and one draw needn't show every extreme that they name: `prompt_length_list`: each row holds the lengths of one group's prompts; a row sums to 512 and its largest entry is exactly 320. `adapter_position`: a permutation of 0 to 63.
All inputs are finite; a program needn't handle non-finite values.
Results may differ from a plain program's by a relative error of at most 0.02.
Values may be sent and summed in bfloat16 or wider, within the bound.
A program may use at most 64 MiB of HBM per device.

v0:
```python
import jax
import jax.numpy as jnp
from jax import lax
from jax.sharding import PartitionSpec as P

HEADS = 8
KV_HEADS = 2
HEAD = 256


ADAPTER_SCALE = 0.5
EPS = 1e-06


def body(
    residual_input,
    queries,
    key_value_pairs,
    prompt_length_list,
    prompt_adapter_index,
    adapter_position,
    output_matrix,
    output_factor_first,
    output_factor_second,
    norm_weight,
    gate_up_matrix,
    gate_up_factor_first,
    gate_up_factor_second,
    down_matrix,
    down_factor_first,
    down_factor_second,
):
    hid_index = lax.axis_index("hid")
    tok_grp = queries.shape[0]
    adapter_list = adapter_position.shape[0]
    rank_width = output_factor_first.shape[2]
    column_shard = residual_input.shape[1]
    group_size = HEADS // KV_HEADS
    key_width = KV_HEADS * HEAD
    wo_rows, gu_rows, down_rows = (
        lax.all_gather(output_matrix, "req", axis=0, tiled=True),
        lax.all_gather(gate_up_matrix, "req", axis=0, tiled=True),
        lax.all_gather(down_matrix, "req", axis=1, tiled=True),
    )
    model_width = gu_rows.shape[0]
    feedforward_shard = gu_rows.shape[2]
    position = jnp.arange(tok_grp, dtype=jnp.int32)
    bounds = jnp.cumsum(prompt_length_list[0])
    segment = jnp.sum((position[:, None] >= bounds[None, :]).astype(jnp.int32), axis=1)
    prompt_hot = (segment[:, None] == jnp.arange(bounds.shape[0], dtype=jnp.int32)[None, :]).astype(
        jnp.int32
    )
    adapter_tok = jnp.sum(prompt_hot * prompt_adapter_index[0][None, :], axis=1)
    adapter_hot = (
        adapter_tok[:, None] == jnp.arange(adapter_list, dtype=jnp.int32)[None, :]
    ).astype(jnp.int32)
    slot_tok = jnp.sum(adapter_hot * adapter_position[None, :], axis=1)
    slot_match = slot_tok[:, None] == jnp.arange(adapter_list, dtype=jnp.int32)[None, :]
    slot_bf = slot_match.astype(jnp.bfloat16)
    slot_float = slot_match.astype(jnp.float32)
    owned = (slot_tok == hid_index).astype(jnp.float32)

    def expand(rank_rows):
        return (slot_bf[:, :, None] * rank_rows[:, None, :]).reshape(
            tok_grp, adapter_list * rank_rows.shape[1]
        )

    query_heads = queries.reshape(tok_grp, KV_HEADS, group_size, HEAD)
    key_rows = key_value_pairs[:, :key_width].reshape(tok_grp, KV_HEADS, HEAD)
    value_rows = key_value_pairs[:, key_width:].reshape(tok_grp, KV_HEADS, HEAD)
    scores = jnp.einsum(
        "tkgd,skd->kgts", query_heads, key_rows, preferred_element_type=jnp.float32
    ) * HEAD ** (-0.5)
    allowed = (segment[:, None] == segment[None, :]) & (position[None, :] <= position[:, None])
    scores = jnp.where(allowed, scores, -1e30)
    attn_probs = jax.nn.softmax(scores, axis=-1).astype(jnp.bfloat16)
    mixed = jnp.einsum("kgts,skd->tkgd", attn_probs, value_rows, preferred_element_type=jnp.float32)
    mixed = mixed.reshape(tok_grp, HEADS * HEAD).astype(jnp.bfloat16)
    wo_both = jnp.concatenate([wo_rows, output_factor_first[0]], axis=1)
    projected = jnp.dot(mixed, wo_both, preferred_element_type=jnp.float32)
    output_primary = projected[:, :column_shard]
    out_part = projected[:, column_shard:] * owned[:, None]
    out_rank = lax.psum(out_part, "hid").astype(jnp.bfloat16)
    output_correction = jnp.dot(
        expand(out_rank),
        output_factor_second.reshape(adapter_list * rank_width, column_shard),
        preferred_element_type=jnp.float32,
    )
    middle_state = (
        residual_input.astype(jnp.float32) + output_primary + ADAPTER_SCALE * output_correction
    ).astype(jnp.bfloat16)
    gu_weight = gu_rows.reshape(model_width, 2 * feedforward_shard)
    gu_factor = gate_up_factor_first[0]
    local = middle_state.astype(jnp.float32)
    squares = lax.psum(jnp.sum(local * local, axis=1), "hid")
    inverse = lax.rsqrt(squares / model_width + EPS)
    normed_part = (local * inverse[:, None] * norm_weight.astype(jnp.float32)[None, :]).astype(
        jnp.bfloat16
    )
    piece = lax.all_gather(normed_part, "hid", axis=1, tiled=True)
    gate_up_joint = jnp.dot(piece, gu_weight, preferred_element_type=jnp.float32)
    gu_part = jnp.dot(piece, gu_factor, preferred_element_type=jnp.float32)
    gate_up_rank = lax.psum(gu_part * owned[:, None], "hid").astype(jnp.bfloat16)
    gate_up_joint = gate_up_joint.reshape(tok_grp, 2, feedforward_shard)
    gate_values = gate_up_joint[:, 0] + ADAPTER_SCALE * jnp.dot(
        expand(gate_up_rank[:, :rank_width]),
        gate_up_factor_second[0].reshape(adapter_list * rank_width, feedforward_shard),
        preferred_element_type=jnp.float32,
    )
    up_projected = gate_up_joint[:, 1] + ADAPTER_SCALE * jnp.dot(
        expand(gate_up_rank[:, rank_width:]),
        gate_up_factor_second[1].reshape(adapter_list * rank_width, feedforward_shard),
        preferred_element_type=jnp.float32,
    )
    hidden_state = (jax.nn.gelu(gate_values, approximate=True) * up_projected).astype(jnp.bfloat16)
    down_complete = jnp.dot(
        hidden_state,
        down_factor_first.reshape(feedforward_shard, adapter_list * rank_width),
        preferred_element_type=jnp.float32,
    )
    down_part = jnp.sum(
        down_complete.reshape(tok_grp, adapter_list, rank_width) * slot_float[:, :, None], axis=1
    )
    down_rank_rows = lax.psum(down_part, "hid").astype(jnp.bfloat16)
    down_correction = jnp.dot(
        expand(down_rank_rows),
        down_factor_second.reshape(adapter_list * rank_width, column_shard),
        preferred_element_type=jnp.float32,
    )
    partial_out = jnp.dot(hidden_state, down_rows, preferred_element_type=jnp.float32)
    feedforward_output = lax.psum_scatter(partial_out, "hid", scatter_dimension=1, tiled=True)
    return (
        middle_state.astype(jnp.float32) + feedforward_output + ADAPTER_SCALE * down_correction
    ).astype(jnp.bfloat16)


def solution(mesh):
    placed = (
        P("req", "hid"),
        P("req", None),
        P("req", None),
        P("req", None),
        P("req", None),
        P(),
        P("req", "hid"),
        P("hid", None, None),
        P(None, None, "hid"),
        P("hid"),
        P("req", None, "hid"),
        P("hid", None, None),
        P(None, None, None, "hid"),
        P("hid", "req"),
        P("hid", None, None),
        P(None, None, "hid"),
    )
    return jax.shard_map(
        body, mesh=mesh, in_specs=placed, out_specs=P("req", "hid"), check_vma=False
    )
```

profile of v0, /device:TPU:1, one launch (start us, length us, event | category | flops | bytes accessed | tf_op | source)
XLA Modules:
  0.0 1018.0 jit_solution(2766046916904005338)
XLA Ops:
  6.5 0.7 all-gather.5.cloned.1.call-update
  7.3 0.0 all-gather.3.cloned.1.call-start
  7.3 0.0 copy-start.13
  7.3 0.0 copy-start.5
  7.3 1.3 fusion.49
  8.6 0.2 copy.63
  8.9 3.3 reshape.134
  12.2 0.2 reduce-window.8
  12.4 0.1 convert_reduce_fusion
  12.5 0.9 fusion.25
  13.4 1.0 copy.51
  14.4 0.1 select_reduce_fusion.1
  14.5 0.3 copy.53
  14.8 1.5 fusion.8
  16.3 5.6 fusion.52
  21.9 0.0 copy-start.8
  21.9 0.0 copy-start.15
  22.0 4.7 fusion.10
  26.7 0.0 copy-start.9
  26.7 0.0 copy-start.2
  26.7 26.8 %all_gather.12 = bf16[2048,32]{0,1:T(8,128)(2,1)S(1)} all-gather(bf16[256,32]{0,1:T(8,128)(2,1)S(1)} %copy-done.12), channel_id=1, replica_groups=mesh['req'=8,'hid'=64] {'req'}, dimensions={0}, use_global_device_ids=true | all-gather | bytes 147456 | tf_op jit(solution)/shard_map/all_gather | solution.py:41
  53.5 0.1 select_reduce_fusion
  53.6 0.5 fusion.38
  54.1 247.1 %psum.28 = bf16[512,16]{0,1:T(8,128)(2,1)S(1)} all-reduce(f32[512,16]{0,1:T(8,128)S(1)} %slice_multiply_fusion), channel_id=1, replica_groups=mesh['req'=8,'hid'=64] {'hid'}, use_global_device_ids=true, to_apply=%region_6.7 | all-reduce | flops 8192 | bytes 49152 | tf_op jit(solution)/shard_map/psum | solution.py:83
  301.2 0.7 fusion.45
  301.9 0.3 multiply_reduce_fusion.1
  302.2 129.1 %psum.29 = f32[512]{0:T(512)S(1)} all-reduce(f32[512]{0:T(512)S(1)} %get-tuple-element.17), channel_id=1, replica_groups=mesh['req'=8,'hid'=64] {'hid'}, use_global_device_ids=true, to_apply=%region_8.9 | all-reduce | flops 512 | bytes 4096 | tf_op jit(solution)/shard_map/psum | solution.py:95
  431.3 0.7 multiply_convert_fusion
  432.0 0.0 all-gather.3.cloned.1.call-update
  432.0 0.0 reduce-scatter.2.cloned.1.call-start
  432.1 20.3 %all_gather.15 = bf16[128,2048]{1,0:T(8,128)(2,1)S(1)} all-gather(bf16[128,256]{1,0:T(8,128)(2,1)S(1)} %copy-done.9), channel_id=1, replica_groups=mesh['req'=8,'hid'=64] {'req'}, dimensions={1}, use_global_device_ids=true | all-gather | bytes 589824 | tf_op jit(solution)/shard_map/all_gather | solution.py:43
  452.4 0.0 all-gather.5.cloned.1.call-done
  452.4 3.7 copy.62
  456.1 54.1 %all-gather.3.cloned.1.call-done = bf16[512,2048]{0,1:T(8,128)(2,1)} async-done(((bf16[512,32]{0,1:T(8,128)(2,1)}), bf16[512,2048]{0,1:T(8,128)(2,1)}) %all-gather.3.cloned.1.call-update) | async-done | bytes 2097168 | tf_op jit(solution)/shard_map/all_gather | solution.py:100
  510.3 2.3 convolution_multiply_fusion.2
  512.5 243.2 %psum.30 = bf16[512,32]{0,1:T(8,128)(2,1)} all-reduce(f32[512,32]{0,1:T(8,128)S(1)} %convolution_multiply_fusion.2), channel_id=1, replica_groups=mesh['req'=8,'hid'=64] {'hid'}, use_global_device_ids=true, to_apply=%region_9.10 | all-reduce | flops 16384 | bytes 98304 | tf_op jit(solution)/shard_map/psum | solution.py:103
  755.7 0.7 fusion.51
  756.5 0.1 broadcast_multiply_fusion
  756.6 2.0 fusion.6
  758.6 0.5 fusion.36
  759.1 0.5 fusion.14
  759.6 0.0 copy-start.6
  759.6 2.7 fusion.53
  762.3 0.0 reduce-scatter.2.cloned.1.call-update
  762.3 0.3 copy.56
  762.6 0.4 multiply_reduce_fusion
  763.1 246.6 %psum.31 = bf16[512,16]{0,1:T(8,128)(2,1)S(1)} all-reduce(f32[512,16]{0,1:T(8,128)S(1)} %multiply_reduce_fusion), channel_id=1, replica_groups=mesh['req'=8,'hid'=64] {'hid'}, use_global_device_ids=true, to_apply=%region_12.13 | all-reduce | flops 8192 | bytes 49152 | tf_op jit(solution)/shard_map/psum | solution.py:124
  1009.7 1.8 fusion.19
  (36 shorter events, 0.1 us)
Async XLA Ops:
  6.5 756.1 %copy-start = (bf16[128,64,16]{0,2,1:T(8,128)(2,1)S(1)}, bf16[128,64,16]{0,2,1:T(8,128)(2,1)}, u32[]{:S(2)}) copy-start(bf16[128,64,16]{0,2,1:T(8,128)(2,1)} %param.30) | copy-start | bytes 786436
  6.5 5.7 copy-start.16
  6.5 445.9 %all-gather.5.cloned.1.call-start = ((), (), s32[]{:S(2)}) async-start(), calls=%async_computation.2 | async-start | bytes 1179648 | tf_op jit(solution)/shard_map/all_gather | solution.py:42
  7.3 503.0 %all-gather.3.cloned.1.call-start = ((), (), s32[]{:S(2)}) async-start(), calls=%async_computation.1 | async-start | bytes 2129920 | tf_op jit(solution)/shard_map/all_gather | solution.py:100
  7.3 7.1 copy-start.13
  7.3 7.1 copy-start.5
  7.3 7.4 copy-start.17
  14.7 1.5 copy-start.4
  16.3 5.6 copy-start.3
  21.9 4.7 copy-start.12
  21.9 31.6 %copy-start.14 = (s32[64]{0:T(128)S(1)}, s32[64]{0:T(128)}, u32[]{:S(2)}) copy-start(s32[64]{0:T(128)} %param.21) | copy-start | bytes 772
  21.9 31.7 %copy-start.8 = (bf16[1,2048,16]{1,2,0:T(8,128)(2,1)S(1)}, bf16[1,2048,16]{1,2,0:T(8,128)(2,1)}, u32[]{:S(2)}) copy-start(bf16[1,2048,16]{1,2,0:T(8,128)(2,1)} %param.23) | copy-start | bytes 196612
  21.9 279.9 %copy-start.15 = (bf16[512,32]{0,1:T(8,128)(2,1)S(1)}, bf16[512,32]{0,1:T(8,128)(2,1)}, u32[]{:S(2)}) copy-start(bf16[512,32]{0,1:T(8,128)(2,1)} %param.16) | copy-start | bytes 98308
  26.7 405.4 %copy-start.9 = (bf16[128,256]{1,0:T(8,128)(2,1)S(1)}, bf16[128,256]{1,0:T(8,128)(2,1)}, u32[]{:S(2)}) copy-start(bf16[128,256]{1,0:T(8,128)(2,1)} %param.29) | copy-start | bytes 196612
  26.7 425.7 %copy-start.2 = (bf16[2,64,16,128]{3,2,1,0:T(8,128)(2,1)S(1)}, bf16[2,64,16,128]{3,2,1,0:T(8,128)(2,1)}, u32[]{:S(2)}) copy-start(bf16[2,64,16,128]{3,2,1,0:T(8,128)(2,1)} %param.28) | copy-start | bytes 1572868
  302.2 129.8 %copy-start.10 = (f32[512,32]{0,1:T(8,128)}, f32[512,32]{0,1:T(8,128)S(1)}, u32[]{:S(2)}) copy-start(f32[512,32]{0,1:T(8,128)S(1)} %get-tuple-element.18) | copy-start | bytes 196612
  432.0 577.7 %reduce-scatter.2.cloned.1.call-start = ((), (), s32[]{:S(2)}) async-start(), calls=%async_computation.3 | async-start | bytes 4259840 | tf_op jit(solution)/shard_map/reduce_scatter | solution.py:131
  510.3 246.3 %copy-start.1 = (bf16[512,2048]{0,1:T(8,128)(2,1)S(1)}, bf16[512,2048]{0,1:T(8,128)(2,1)}, u32[]{:S(2)}) copy-start(bf16[512,2048]{0,1:T(8,128)(2,1)} %all-gather.3.cloned.1.call-done) | copy-start | bytes 6291460
  759.6 2.7 copy-start.6
  759.6 3.0 copy-start.7
  762.3 247.4 %copy-start.11 = (f32[512,32]{0,1:T(8,128)S(1)}, f32[512,32]{0,1:T(8,128)}, u32[]{:S(2)}) copy-start(f32[512,32]{0,1:T(8,128)} %copy-done.10) | copy-start | bytes 196612
Sparse Core Ops, SparseCore 0:
  9.4 43.1 all-gather.4
  432.1 78.1 all-gather.2
  762.4 150.6 reduce-scatter.1
where the time goes:
time: 1020 us
  blocking collectives  913 us (90%)
  waiting for transfers between devices  54.9 us (5%)
  matrix products  17.1 us (2%)
  between operations  13.4 us (1%)
  local copies, waits for them, and re-layouts  10.9 us (1%)
    psum x1, blocking collectives, body(): out_rank = lax.psum(out_part, 'hid').astype(jnp.bfloat16)  247 us
    psum x1, blocking collectives, body(): down_rank_rows = lax.psum(down_part, 'hid').astype(jnp.bfloat16)  247 us
    psum x1, blocking collectives, body(): lax.psum(gu_part * owned[:, None], 'hid').astype(jnp.bfloat16)  243 us
    psum x1, blocking collectives, body(): squares = lax.psum(jnp.sum(local * local, axis=1), 'hid')  129 us
    all_gather x1, waiting for transfers between devices, body(): piece = lax.all_gather(normed_part, 'hid', axis=1, tiled=True)  54.1 us
    all_gather x1, blocking collectives, body(): lax.all_gather(output_matrix, 'req', axis=0, tiled=True)  26.8 us
  transfers between devices with their start and end apart: 3, of which 1 were waited for; matrix products, arithmetic and copies ran while one was open for 3% of the time, Pallas kernels for 0%

commit v1 on v0

v1 whole, which is shorter than its diff:
```python
import functools

import jax
import jax.numpy as jnp
from jax import lax
from jax.experimental import pallas as pl
from jax.experimental.pallas import tpu as pltpu
from jax.sharding import PartitionSpec as P

HEADS = 8
KV_HEADS = 2
HEAD = 256
CHUNK = 32
CORES = 2
GRID_X = 4
ADAPTER_SCALE = 0.5
EPS = 1e-06

MESH = pl.DeviceIdType.MESH
F32 = jnp.float32
BF16 = jnp.bfloat16


def dot(a, b):
    return jnp.dot(a, b, preferred_element_type=F32)


def token_bounds(lengths_ref, count):
    bounds, total = [], 0
    for p in range(count):
        start = total
        total = total + lengths_ref[0, p]
        bounds.append((start, total))
    return bounds


def attention_kernel(prompts, lengths_ref, q_ref, k_ref, v_ref, out_ref):
    tokens = q_ref.shape[0]
    half = tokens // 2
    column = lax.broadcasted_iota(jnp.int32, (1, tokens), 1)
    first = jnp.zeros((1, tokens), jnp.int32)
    for start, _ in token_bounds(lengths_ref, prompts):
        first = jnp.where(column >= start, start, first)
    values = v_ref[...].astype(F32).T.astype(BF16)
    for block in range(2):
        lo, hi = block * half, (block + 1) * half
        scores = lax.dot_general(
            k_ref[:hi, :], q_ref[lo:hi, :], (((1,), (1,)), ((), ())), preferred_element_type=F32
        )
        row = lax.broadcasted_iota(jnp.int32, (hi, half), 0)
        allowed = (row >= first[:, lo:hi]) & (row <= column[:, lo:hi])
        scores = jnp.where(allowed, scores * HEAD ** (-0.5), -1e30)
        top = jnp.max(scores, axis=0, keepdims=True)
        weights = jnp.exp(scores - top)
        total = jnp.sum(weights, axis=0, keepdims=True)
        mixed = dot(values[:, :hi], weights.astype(BF16))
        out_ref[:, lo:hi] = (mixed / total).astype(BF16)


def attention(queries, pairs, lengths):
    tokens = queries.shape[0]
    heads = queries.shape[1] // HEAD
    kv_heads = pairs.shape[1] // (2 * HEAD)
    group = heads // kv_heads
    return pl.pallas_call(
        functools.partial(attention_kernel, lengths.shape[1]),
        grid=(heads,),
        out_shape=jax.ShapeDtypeStruct((heads * HEAD, tokens), BF16),
        in_specs=[
            pl.BlockSpec(memory_space=pltpu.SMEM),
            pl.BlockSpec((tokens, HEAD), lambda h: (0, h)),
            pl.BlockSpec((tokens, HEAD), lambda h: (0, h // group)),
            pl.BlockSpec((tokens, HEAD), lambda h: (0, kv_heads + h // group)),
        ],
        out_specs=pl.BlockSpec((HEAD, tokens), lambda h: (h, 0)),
    )(lengths, queries, pairs, pairs)


class Sems:
    def __init__(self, send, recv, used=0):
        self.send, self.recv, self.used = send, recv, used

    def reserve(self, count):
        part = Sems(self.send, self.recv, self.used)
        self.used += count
        return part

    def again(self):
        return Sems(self.send, self.recv, self.used)

    def take(self):
        n = self.used
        self.used += 1
        return self.send.at[n], self.recv.at[n]


SEMAPHORES = 400


def main_kernel(
    dims,
    lengths_ref,
    adapters_ref,
    places_ref,
    attn_ref,
    residual_ref,
    gain_ref,
    wo_ref,
    ao_ref,
    bo_ref,
    gate_ref,
    up_ref,
    agu_ref,
    bgu_ref,
    down_ref,
    ad_ref,
    bd_ref,
    out_ref,
    wo_all,
    gu_all,
    down_all,
    gathered,
    normed,
    partial,
    pair_in,
    summed,
    ring_out,
    ring_in,
    cross_in,
    last_out,
    last_in,
    rank_pair,
    rank_x,
    rank_xin,
    rank_yin,
    rank_back,
    gu_pair,
    gu_x,
    gu_xin,
    gu_yin,
    gu_back,
    sq_pair,
    sq_x,
    sq_xin,
    sq_yin,
    sq_back,
    down_pair,
    down_x,
    down_xin,
    down_yin,
    down_back,
    send_sems,
    recv_sems,
):
    zs, ys, xs = dims
    tokens = attn_ref.shape[1]
    half = tokens // 2
    width = attn_ref.shape[0]
    prompts = lengths_ref.shape[1]
    z = lax.axis_index("req")
    me = lax.axis_index("hid")
    c = lax.rem(me, CORES)
    x = lax.rem(me // CORES, xs)
    y = me // (CORES * xs)
    sems = Sems(send_sems, recv_sems)

    def at(yy, xx, cc):
        return (z, yy * (xs * CORES) + xx * CORES + cc)

    def mod(value, size):
        return lax.rem(value + size, size)

    partner = at(y, x, 1 - c)

    def to_x(k):
        return at(y, mod(x + k, xs), c)

    def to_y(k):
        return at(mod(y + k, ys), x, c)

    def to_z(k):
        return (mod(z + k, zs), me)

    def copy(src, dst, pair, device):
        made = pltpu.make_async_remote_copy(
            src_ref=src,
            dst_ref=dst,
            send_sem=pair[0],
            recv_sem=pair[1],
            device_id=device,
            device_id_type=MESH,
        )
        return made

    def send(src, dst, pair, device):
        made = copy(src, dst, pair, device)
        made.start()
        return made

    def arrived(dst, pair):
        copy(dst, dst, pair, partner).wait_recv()

    barrier = pltpu.get_barrier_semaphore()
    peers = [partner]
    peers += [to_x(k) for k in range(1, xs)]
    peers += [to_y(k) for k in range(1, ys)]
    peers += [to_z(k) for k in range(1, zs)]
    for peer in peers:
        pl.semaphore_signal(barrier, inc=1, device_id=peer, device_id_type=MESH)

    wo_all[z] = wo_ref[...]
    hidden = gate_ref.shape[1]
    gu_all[z, 0:hidden, :] = gate_ref[...].astype(F32).T.astype(BF16)
    gu_all[z, hidden : 2 * hidden, :] = up_ref[...].astype(F32).T.astype(BF16)
    down_all[z] = down_ref[...].astype(F32).T.astype(BF16)

    column = lax.broadcasted_iota(jnp.int32, (1, tokens), 1)
    slots, members = [], []
    owned = jnp.zeros((1, tokens), F32)
    slot_row = jnp.zeros((1, tokens), jnp.int32)
    for p, (start, stop) in enumerate(token_bounds(lengths_ref, prompts)):
        slot = places_ref[adapters_ref[0, p]]
        inside = (column >= start) & (column < stop)
        slots.append(slot)
        members.append(inside.astype(F32))
        owned = owned + jnp.where(inside, jnp.where(slot == me, 1.0, 0.0), 0.0)
        slot_row = jnp.where(inside, slot, slot_row)
    adapters = bo_ref.shape[2]
    chosen = (lax.broadcasted_iota(jnp.int32, (adapters, tokens), 0) == slot_row).astype(BF16)

    pl.semaphore_wait(barrier, len(peers))

    pending = []
    places = [mod(z + k, zs) for k in range(zs)]
    wo_pairs = [sems.take() for _ in range(zs - 1)]
    for k in range(1, zs):
        pending.append(send(wo_all.at[z], wo_all.at[z], wo_pairs[k - 1], to_z(k)))
    ups, downs = zs // 2, (zs - 1) // 2
    z_pairs = {}
    for way, hops in ((1, ups), (-1, downs)):
        for hop in range(1, hops + 1):
            z_pairs[way, hop] = (sems.take(), sems.take())

    def z_slot(way, hop):
        return (zs - way * hop) % zs

    def z_wait(hop):
        for way, hops in ((1, ups), (-1, downs)):
            if 1 <= hop <= hops:
                k = z_slot(way, hop)
                arrived(gu_all.at[places[k]], z_pairs[way, hop][0])
                arrived(down_all.at[places[k]], z_pairs[way, hop][1])

    def z_step(hop):
        z_wait(hop - 1)
        for way, hops in ((1, ups), (-1, downs)):
            if hop <= hops:
                k = z_slot(way, hop - 1)
                block = gu_all.at[places[k]]
                pending.append(send(block, block, z_pairs[way, hop][0], to_z(way)))
                block = down_all.at[places[k]]
                pending.append(send(block, block, z_pairs[way, hop][1], to_z(way)))

    z_step(1)

    def all_reduce(value, pair_buf, x_buf, xin, yin, back, fillers=()):
        fillers = list(fillers) + [lambda: None] * 4
        kind = pair_buf.dtype
        pair_buf[0] = value[:, :half].astype(kind)
        pair_buf[1] = value[:, half:].astype(kind)
        pair = sems.take()
        first = send(pair_buf.at[1 - c], pair_buf.at[2], pair, partner)
        pending.append(first)
        fillers[0]()
        arrived(pair_buf.at[2], pair)
        total = pair_buf[c].astype(F32) + pair_buf[2].astype(F32)
        x_buf[0] = total.astype(kind)
        pairs = [sems.take() for _ in range(1, xs)]
        for k in range(1, xs):
            pending.append(send(x_buf.at[0], xin.at[k - 1], pairs[k - 1], to_x(k)))
        fillers[1]()
        for k in range(1, xs):
            arrived(xin.at[k - 1], pairs[k - 1])
            total = total + xin[k - 1].astype(F32)
        x_buf[1] = total.astype(kind)
        pairs = [sems.take() for _ in range(1, ys)]
        for k in range(1, ys):
            pending.append(send(x_buf.at[1], yin.at[k - 1], pairs[k - 1], to_y(k)))
        fillers[2]()
        for k in range(1, ys):
            arrived(yin.at[k - 1], pairs[k - 1])
            total = total + yin[k - 1].astype(F32)
        back[c] = total.astype(kind)
        pair = sems.take()
        pending.append(send(back.at[c], back.at[c], pair, partner))
        fillers[3]()
        arrived(back.at[1 - c], pair)
        return jnp.concatenate([back[0], back[1]], axis=1)

    def expand(rank):
        return jnp.concatenate([rank * members[p] for p in range(prompts)], axis=0).astype(BF16)

    def column_correction(b_ref, rank):
        ranks = b_ref.shape[0]
        picked = dot(b_ref[...].reshape(ranks * CHUNK, adapters), chosen)
        total = jnp.zeros((CHUNK, tokens), F32)
        for r in range(ranks):
            total = total + picked[r * CHUNK : (r + 1) * CHUNK] * rank[r : r + 1]
        return total

    attn = attn_ref[...]
    out_part = dot(ao_ref[...], attn) * owned
    held = {}

    def project():
        for k in range(1, zs):
            arrived(wo_all.at[places[zs - k]], wo_pairs[k - 1])
        weights = jnp.concatenate([wo_all[k] for k in range(zs)], axis=1)
        held["main"] = dot(weights, attn)

    out_rank = all_reduce(
        out_part, rank_pair, rank_x, rank_xin, rank_yin, rank_back, [None or (lambda: None), lambda: z_step(2), project]
    ).astype(F32)
    middle = (
        residual_ref[...].astype(F32)
        + held["main"]
        + ADAPTER_SCALE * column_correction(bo_ref, out_rank)
    ).astype(BF16)
    local = middle.astype(F32)
    gain_row = gain_ref[...].astype(F32)
    diagonal = lax.broadcasted_iota(jnp.int32, (CHUNK, CHUNK), 0) == lax.broadcasted_iota(
        jnp.int32, (CHUNK, CHUNK), 1
    )
    gain = jnp.sum(jnp.where(diagonal, gain_row, 0.0), axis=1, keepdims=True)
    gathered[c, y, x] = (local * gain).astype(BF16)

    hops_up, hops_down = ys // 2, (ys - 1) // 2
    branch_copies = max(xs - 1 + xs * (hops_up + hops_down), ys - 1 + ys * (xs - 1))
    row_pairs = [sems.take() for _ in range(ys)]
    gather_sems = sems.reserve(branch_copies)

    def gather_zero():
        sems = gather_sems.again()
        own = gathered.at[0, y, x]
        x_pairs = [None] + [sems.take() for _ in range(1, xs)]
        ring = {
            (way, hop, j): sems.take()
            for way, hops in ((1, hops_up), (-1, hops_down))
            for hop in range(1, hops + 1)
            for j in range(xs)
        }
        sent = []
        for k in range(1, xs):
            sent.append(send(own, own, x_pairs[k], to_x(k)))
        for hop in range(1, max(hops_up, hops_down) + 2):
            for j in range(xs):
                xj = mod(x - j, xs)
                if hop == 1 and j > 0:
                    arrived(gathered.at[0, y, xj], x_pairs[j])
                for way, hops in ((1, hops_up), (-1, hops_down)):
                    block = gathered.at[0, mod(y - way * (hop - 1), ys), xj]
                    if 1 < hop <= hops + 1:
                        arrived(block, ring[way, hop - 1, j])
                    if hop <= hops:
                        sent.append(send(block, block, ring[way, hop, j], to_y(way)))
            ways = (1,) if hop == 1 else (1, -1)
            for way in ways:
                if hop == 1 or hop - 1 <= (hops_up if way == 1 else hops_down):
                    k = (way * (hop - 1)) % ys
                    block = gathered.at[0, mod(y - k, ys)]
                    sent.append(send(block, block, row_pairs[k], partner))
        for made in sent:
            made.wait_send()

    def gather_one():
        sems = gather_sems.again()
        own = gathered.at[1, y, x]
        y_pairs = [None] + [sems.take() for _ in range(1, ys)]
        x_pairs = {(r, k): sems.take() for r in range(ys) for k in range(1, xs)}
        sent = []
        order = sorted(range(ys), key=lambda k: min(k, ys - k))
        for k in order[1:]:
            sent.append(send(own, own, y_pairs[k], to_y(k)))
        for r in order:
            block = gathered.at[1, mod(y - r, ys), x]
            if r > 0:
                arrived(block, y_pairs[r])
            for k in range(1, xs):
                sent.append(send(block, block, x_pairs[r, k], to_x(k)))
        for r in order:
            for k in range(1, xs):
                arrived(gathered.at[1, mod(y - r, ys), mod(x - k, xs)], x_pairs[r, k])
            block = gathered.at[1, mod(y - r, ys)]
            sent.append(send(block, block, row_pairs[r], partner))
        for made in sent:
            made.wait_send()

    def run_gather():
        pl.when(c == 0)(gather_zero)
        pl.when(c == 1)(gather_one)
        for k in range(ys):
            arrived(gathered.at[1 - c, mod(y - k, ys)], row_pairs[k])

    squares = jnp.broadcast_to(jnp.sum(local * local, axis=0, keepdims=True), (8, tokens))
    squares = all_reduce(
        squares, sq_pair, sq_x, sq_xin, sq_yin, sq_back, [lambda: None, lambda: z_step(3), run_gather]
    )[0:1]
    inverse = lax.rsqrt(squares / width + EPS)
    z_step(4)
    per_row = width // ys
    for row in range(ys):
        for col in range(xs):
            for core in range(CORES):
                top = row * per_row + (col * CORES + core) * CHUNK
                block = gathered[core, row, col].astype(F32) * inverse
                normed[top : top + CHUNK, :] = block.astype(BF16)

    gu_part = dot(agu_ref[...], normed[...]) * owned

    def gate_up():
        for hop in range(5, max(ups, downs) + 1):
            z_step(hop)
        z_wait(max(ups, downs))
        weights = jnp.concatenate([gu_all[k] for k in range(zs)], axis=1)
        held["gu"] = dot(weights, normed[...])

    gu_rank = all_reduce(
        gu_part, gu_pair, gu_x, gu_xin, gu_yin, gu_back, [lambda: None, lambda: None, gate_up]
    ).astype(F32)
    ranks = gu_rank.shape[0] // 2

    def hidden_correction(which, rank):
        rows = jnp.concatenate([bgu_ref[which, slot] for slot in slots], axis=0)
        return ADAPTER_SCALE * dot(rows.astype(F32).T.astype(BF16), expand(rank))

    gate = held["gu"][:hidden] + hidden_correction(0, gu_rank[:ranks])
    up = held["gu"][hidden:] + hidden_correction(1, gu_rank[ranks:])
    hidden_state = (jax.nn.gelu(gate, approximate=True) * up).astype(BF16)

    a_rows = jnp.concatenate([ad_ref[slot] for slot in slots], axis=0)
    shares = dot(a_rows, hidden_state)
    down_part = jnp.zeros((ranks, tokens), F32)
    for p in range(prompts):
        down_part = down_part + shares[p * ranks : (p + 1) * ranks] * members[p]

    result = {}

    def scatter_pairs():
        pairs = [sems.take() for _ in range(ys)]
        weights = down_all[...].reshape(width, hidden)
        for row in range(ys):
            block = dot(weights[row * per_row : (row + 1) * per_row], hidden_state).astype(BF16)
            partial[row] = block.reshape(xs, CORES, CHUNK, tokens)
            pending.append(send(partial.at[row, :, 1 - c], pair_in.at[row], pairs[row], partner))
        for row in range(ys):
            arrived(pair_in.at[row], pairs[row])
            summed[row] = (partial[row, :, c].astype(F32) + pair_in[row].astype(F32)).astype(BF16)

    scatter_sems = sems.reserve(branch_copies)

    def scatter_zero():
        sems = scatter_sems.again()
        ring = {
            (way, hop, j): sems.take()
            for way, hops in ((1, hops_up), (-1, hops_down))
            for hop in range(1, hops + 1)
            for j in range(xs)
        }
        x_pairs = [None] + [sems.take() for _ in range(1, xs)]
        slot_of = {}
        for way, hops in ((1, hops_up), (-1, hops_down)):
            for hop in range(1, hops + 1):
                slot_of[way, hop] = len(slot_of)
        sent = []
        for hop in range(1, max(hops_up, hops_down) + 1):
            for j in range(xs):
                for way, hops in ((1, hops_up), (-1, hops_down)):
                    if hop > hops:
                        continue
                    row = mod(y + way * (hops + 1 - hop), ys)
                    n = slot_of[way, hop]
                    if hop == 1:
                        block = summed.at[row, j]
                    else:
                        before = slot_of[way, hop - 1]
                        arrived(ring_in.at[before, j], ring[way, hop - 1, j])
                        total = summed[row, j].astype(F32) + ring_in[before, j].astype(F32)
                        ring_out[n, j] = total.astype(BF16)
                        block = ring_out.at[n, j]
                    sent.append(send(block, ring_in.at[n, j], ring[way, hop, j], to_y(way)))
        for j in range(xs):
            total = summed[y, j].astype(F32)
            for way, hops in ((1, hops_up), (-1, hops_down)):
                if hops > 0:
                    n = slot_of[way, hops]
                    arrived(ring_in.at[n, j], ring[way, hops, j])
                    total = total + ring_in[n, j].astype(F32)
            last_out[j] = total.astype(BF16)
        for k in range(1, xs):
            sent.append(send(last_out.at[mod(x + k, xs)], last_in.at[k], x_pairs[k], to_x(k)))
        total = last_out[x].astype(F32)
        for k in range(1, xs):
            arrived(last_in.at[k], x_pairs[k])
            total = total + last_in[k].astype(F32)
        last_in[0] = total.astype(BF16)
        for made in sent:
            made.wait_send()

    def scatter_one():
        sems = scatter_sems.again()
        x_pairs = {(r, k): sems.take() for r in range(ys) for k in range(1, xs)}
        y_pairs = [None] + [sems.take() for _ in range(1, ys)]
        sent = []
        order = sorted(range(ys), key=lambda k: -min(k, ys - k))
        for r in order:
            row = mod(y + r, ys)
            for k in range(1, xs):
                sent.append(
                    send(summed.at[row, mod(x + k, xs)], cross_in.at[r, k - 1], x_pairs[r, k], to_x(k))
                )
        for r in order:
            total = summed[mod(y + r, ys), x].astype(F32)
            for k in range(1, xs):
                arrived(cross_in.at[r, k - 1], x_pairs[r, k])
                total = total + cross_in[r, k - 1].astype(F32)
            last_out[r] = total.astype(BF16)
            if r > 0:
                sent.append(send(last_out.at[r], last_in.at[r], y_pairs[r], to_y(r)))
        total = last_out[0].astype(F32)
        for r in range(1, ys):
            arrived(last_in.at[r], y_pairs[r])
            total = total + last_in[r].astype(F32)
        last_in[0] = total.astype(BF16)
        for made in sent:
            made.wait_send()

    def run_scatter():
        pl.when(c == 0)(scatter_zero)
        pl.when(c == 1)(scatter_one)

    down_rank = all_reduce(
        down_part,
        down_pair,
        down_x,
        down_xin,
        down_yin,
        down_back,
        [scatter_pairs, lambda: None, run_scatter],
    ).astype(F32)
    down_rank = down_rank.astype(BF16).astype(F32)
    out_ref[...] = (
        middle.astype(F32)
        + last_in[0].astype(F32)
        + ADAPTER_SCALE * column_correction(bd_ref, down_rank)
    ).astype(BF16)
    for made in pending:
        made.wait_send()


def main_call(dims, args):
    zs, ys, xs = dims
    attn = args[3]
    tokens = attn.shape[1]
    width = attn.shape[0]
    half = tokens // 2
    gate = args[9]
    hidden = gate.shape[1]
    span = gate.shape[0]
    down_cols = args[13].shape[1]
    ranks = args[7].shape[0]
    hops = ys // 2 + (ys - 1) // 2
    plane = (ys, xs, CORES, CHUNK, tokens)

    def reduce_buffers(rows, kind):
        return [
            pltpu.VMEM((3, rows, half), kind),
            pltpu.VMEM((2, rows, half), kind),
            pltpu.VMEM((max(xs - 1, 1), rows, half), kind),
            pltpu.VMEM((ys - 1, rows, half), kind),
            pltpu.VMEM((2, rows, half), kind),
        ]

    scratch = [
        pltpu.VMEM((zs, CHUNK, span), BF16),
        pltpu.VMEM((zs, 2 * hidden, span), BF16),
        pltpu.VMEM((zs, down_cols, hidden), BF16),
        pltpu.VMEM((CORES, ys, xs, CHUNK, tokens), BF16),
        pltpu.VMEM((width, tokens), BF16),
        pltpu.VMEM(plane, BF16),
        pltpu.VMEM((ys, xs, CHUNK, tokens), BF16),
        pltpu.VMEM((ys, xs, CHUNK, tokens), BF16),
        pltpu.VMEM((hops, xs, CHUNK, tokens), BF16),
        pltpu.VMEM((hops, xs, CHUNK, tokens), BF16),
        pltpu.VMEM((ys, xs - 1, CHUNK, tokens), BF16),
        pltpu.VMEM((max(xs, ys), CHUNK, tokens), BF16),
        pltpu.VMEM((max(xs, ys), CHUNK, tokens), BF16),
    ]
    scratch += reduce_buffers(ranks, BF16)
    scratch += reduce_buffers(2 * ranks, BF16)
    scratch += reduce_buffers(8, F32)
    scratch += reduce_buffers(ranks, F32)
    scratch += [pltpu.SemaphoreType.DMA((SEMAPHORES,)), pltpu.SemaphoreType.DMA((SEMAPHORES,))]
    smem = pl.BlockSpec(memory_space=pltpu.SMEM)
    vmem = pl.BlockSpec(memory_space=pltpu.VMEM)
    return pl.pallas_call(
        functools.partial(main_kernel, dims),
        out_shape=jax.ShapeDtypeStruct((CHUNK, tokens), BF16),
        in_specs=[smem] * 3 + [vmem] * (len(args) - 3),
        out_specs=vmem,
        scratch_shapes=scratch,
        compiler_params=pltpu.CompilerParams(
            collective_id=0, has_side_effects=True, vmem_limit_bytes=60 * 1024 * 1024
        ),
    )(*args)


def body(
    dims,
    residual_input,
    queries,
    key_value_pairs,
    prompt_length_list,
    prompt_adapter_index,
    adapter_position,
    output_matrix,
    output_factor_first,
    output_factor_second,
    norm_weight,
    gate_up_matrix,
    gate_up_factor_first,
    gate_up_factor_second,
    down_matrix,
    down_factor_first,
    down_factor_second,
):
    attn = attention(queries, key_value_pairs, prompt_length_list)
    args = [
        prompt_length_list,
        prompt_adapter_index,
        adapter_position,
        attn,
        residual_input.T,
        norm_weight.reshape(1, -1),
        output_matrix.T,
        output_factor_first[0].T,
        output_factor_second.transpose(1, 2, 0),
        gate_up_matrix[:, 0, :],
        gate_up_matrix[:, 1, :],
        gate_up_factor_first[0].T,
        gate_up_factor_second,
        down_matrix,
        down_factor_first.transpose(1, 2, 0),
        down_factor_second.transpose(1, 2, 0),
    ]
    return main_call(dims, args).T


def solution(mesh):
    placed = (
        P("req", "hid"),
        P("req", None),
        P("req", None),
        P("req", None),
        P("req", None),
        P(),
        P("req", "hid"),
        P("hid", None, None),
        P(None, None, "hid"),
        P("hid"),
        P("req", None, "hid"),
        P("hid", None, None),
        P(None, None, None, "hid"),
        P("hid", "req"),
        P("hid", None, None),
        P(None, None, "hid"),
    )
    dims = (mesh.shape["req"], mesh.shape["hid"] // (CORES * GRID_X), GRID_X)
    return jax.shard_map(
        functools.partial(body, dims),
        mesh=mesh,
        in_specs=placed,
        out_specs=P("req", "hid"),
        check_vma=False,
    )
```

time: 1020 us -> 121 us (0.12)
  blocking collectives: 913 us -> 0 us
  Pallas kernels: 0 us -> 117 us
  waiting for transfers between devices: 54.9 us -> 0 us
  matrix products: 17.1 us -> 0 us
  between operations: 13.4 us -> 0.01 us
    psum x4 -> x0, blocking collectives: 866 us -> none  [the longest x1 247 us: body(): out_rank = lax.psum(out_part, 'hid').astype(jnp.bfloat16)]
    pallas_call x0 -> x2, Pallas kernels: none -> 117 us  [the longest x1 107 us: main_call(): pl.pallas_call(functools.partial(main_kernel, dims), out_shape=jax.ShapeD...]
    all_gather x2 -> x0, waiting for transfers between devices: 54.1 us -> none  [the longest x1 54.1 us: body(): piece = lax.all_gather(normed_part, 'hid', axis=1, tiled=True)]
    all_gather x2 -> x0, blocking collectives: 47.1 us -> none  [the longest x1 26.8 us: body(): lax.all_gather(output_matrix, 'req', axis=0, tiled=True)]
    dot_general x11 -> x0, matrix products: 17.1 us -> none  [the longest x1 4.69 us: body(): jnp.einsum('kgts,skd->tkgd', attn_probs, value_rows, preferred_element_ty...]
  transfers between devices with their start and end apart: 3 -> 0, of which waited for: 1 -> 0; matrix products, arithmetic and copies ran while one was open for 3% -> 0% of each run, Pallas kernels for 0% -> 0%
where the time goes in v1:
time: 121 us
  Pallas kernels  117 us (97%)
  local copies, waits for them, and re-layouts  3.26 us (3%)
    pallas_call x1, Pallas kernels, main_call(): pl.pallas_call(functools.partial(main_kernel, dims), out_shape=jax.ShapeD...  107 us
    pallas_call x1, Pallas kernels, attention(): pl.pallas_call(functools.partial(attention_kernel, lengths.shape[1]), gri...  10.1 us

profile of v1, /device:TPU:1, one launch (start us, length us, event | category | flops | bytes accessed | tf_op | source)
XLA Modules:
  0.0 120.6 jit_solution(575114813467758253)
XLA Ops:
  0.0 1.2 fusion
  1.2 0.7 copy_bitcast_fusion
  1.9 10.1 %shard_map.154.attn_ref = bf16[2048,512]{1,0:T(8,128)(2,1)} custom-call(s32[1,6]{1,0:T(1,128)} %lengths_ref.3, bf16[512,2048]{1,0:T(8,128)(2,1)} %q_ref.1, bf16[512,1024]{1,0:T(8,128)(2,1)} %v_ref.1, bf16[512,1024]{1,0:T(8,128)(2,1)} %v_ref.1), custom_call_target="tpu_custom_call" | custom-call | tf_op jit(solution)/shard_map/pallas_call | solution.py:65
  11.9 107.2 %shard_map.155 = bf16[32,512]{1,0:T(8,128)(2,1)} custom-call(s32[1,6]{1,0:T(1,128)} %lengths_ref.3, s32[1,6]{1,0:T(1,128)} %adapters_ref.1, s32[64]{0:T(128)} %places_ref.1, bf16[2048,512]{1,0:T(8,128)(2,1)} %shard_map.154.attn_ref, bf16[32,512]{1,0:T(8,128)(2,1)} %bitcast.23, bf16[1,32]{1,0:T(2,128)(2,1)} %bitcast.25, bf16[32,256]{1,0:T(8,128)(2,1)} %bitcast.24, ...), custom_call_target="tpu_custom_call" | custom-call | tf_op jit(solution)/shard_map/pallas_call | solution.py:605
  119.2 1.4 %copy.24 = bf16[512,32]{0,1:T(8,128)(2,1)} copy(bf16[512,32]{0,1:T(8,128)(2,1)} %bitcast.18) | data formatting | bytes 65536

commit v2 on v1

v2 whole, which is shorter than its diff:
```python
import functools

import jax
import jax.numpy as jnp
from jax import lax
from jax.experimental import pallas as pl
from jax.experimental.pallas import tpu as pltpu
from jax.sharding import PartitionSpec as P

HEADS = 8
KV_HEADS = 2
HEAD = 256
CHUNK = 32
CORES = 2
GRID_X = 4
ADAPTER_SCALE = 0.5
EPS = 1e-06

MESH = pl.DeviceIdType.MESH
F32 = jnp.float32
BF16 = jnp.bfloat16


def dot(a, b):
    return jnp.dot(a, b, preferred_element_type=F32)


def token_bounds(lengths_ref, count):
    bounds, total = [], 0
    for p in range(count):
        start = total
        total = total + lengths_ref[0, p]
        bounds.append((start, total))
    return bounds


class Sems:
    def __init__(self, send, recv, used=0):
        self.send, self.recv, self.used = send, recv, used

    def reserve(self, count):
        part = Sems(self.send, self.recv, self.used)
        self.used += count
        return part

    def again(self):
        return Sems(self.send, self.recv, self.used)

    def take(self):
        n = self.used
        self.used += 1
        return self.send.at[n], self.recv.at[n]


SEMAPHORES = 400


def main_kernel(
    dims,
    lengths_ref,
    adapters_ref,
    places_ref,
    queries_ref,
    pairs_ref,
    residual_ref,
    gain_ref,
    wo_ref,
    ao_ref,
    bo_ref,
    gate_ref,
    up_ref,
    agu_ref,
    bgu_ref,
    down_ref,
    ad_ref,
    bd_ref,
    out_ref,
    q_all,
    kv_all,
    values_all,
    attn_all,
    wo_all,
    gu_all,
    down_all,
    factors,
    middle_ref,
    gathered,
    normed,
    partial,
    pair_in,
    summed,
    ring_out,
    ring_in,
    cross_in,
    last_out,
    last_in,
    rank_pair,
    rank_x,
    rank_xin,
    rank_yin,
    rank_back,
    gu_pair,
    gu_x,
    gu_xin,
    gu_yin,
    gu_back,
    local_sems,
    send_sems,
    recv_sems,
):
    zs, ys, xs = dims
    heads, tokens, _ = q_all.shape
    kv_heads = values_all.shape[0]
    group = heads // kv_heads
    half = tokens // 2
    width = attn_all.shape[0]
    prompts = lengths_ref.shape[1]
    ranks = ao_ref.shape[0]
    z = lax.axis_index("req")
    me = lax.axis_index("hid")
    c = lax.rem(me, CORES)
    x = lax.rem(me // CORES, xs)
    y = me // (CORES * xs)
    sems = Sems(send_sems, recv_sems)
    pending = []

    def at(yy, xx, cc):
        return (z, yy * (xs * CORES) + xx * CORES + cc)

    def mod(value, size):
        return lax.rem(value + size, size)

    def partner():
        return at(y, x, 1 - c)

    def to_x(k):
        return at(y, mod(x + k, xs), c)

    def to_y(k):
        return at(mod(y + k, ys), x, c)

    def to_z(k):
        return (mod(z + k, zs), me)

    def copy(src, dst, pair, device):
        return pltpu.make_async_remote_copy(
            src_ref=src,
            dst_ref=dst,
            send_sem=pair[0],
            recv_sem=pair[1],
            device_id=device,
            device_id_type=MESH,
        )

    def send(src, dst, pair, device):
        made = copy(src, dst, pair, device)
        made.start()
        return made

    def arrived(dst, pair):
        copy(dst, dst, pair, partner()).wait_recv()

    def launch(make):
        make().start()
        pending.append(make)

    loads = []
    for n in range(2 * kv_heads):
        loads.append(
            pltpu.make_async_copy(
                pairs_ref.at[:, n * HEAD : (n + 1) * HEAD], kv_all.at[n], local_sems.at[n]
            )
        )
    for h in range(heads):
        loads.append(
            pltpu.make_async_copy(
                queries_ref.at[:, h * HEAD : (h + 1) * HEAD],
                q_all.at[h],
                local_sems.at[2 * kv_heads + h],
            )
        )
    for load in loads:
        load.start()

    barrier = pltpu.get_barrier_semaphore()
    peers = [partner()]
    peers += [to_x(k) for k in range(1, xs)]
    peers += [to_y(k) for k in range(1, ys)]
    peers += [to_z(k) for k in range(1, zs)]
    for peer in peers:
        pl.semaphore_signal(barrier, inc=1, device_id=peer, device_id_type=MESH)

    wo_all[z] = wo_ref[...]
    hidden = gate_ref.shape[1]
    down_cols = down_ref.shape[1]
    gu_all[z, 0:hidden, :] = gate_ref[...].astype(F32).T.astype(BF16)
    gu_all[z, hidden : 2 * hidden, :] = up_ref[...].astype(F32).T.astype(BF16)
    down_rows = pl.ds(pl.multiple_of(z * down_cols, down_cols), down_cols)
    down_all[down_rows, :] = down_ref[...].astype(F32).T.astype(BF16)

    column = lax.broadcasted_iota(jnp.int32, (1, tokens), 1)
    adapters = bo_ref.shape[2]
    lane = lax.broadcasted_iota(jnp.int32, (1, 128), 1)
    slots, members = [], []
    owned = jnp.zeros((1, tokens), F32)
    first = jnp.zeros((1, tokens), jnp.int32)
    slot_lane = jnp.full((1, 128), -1, jnp.int32)
    total = 0
    for p in range(prompts):
        start = total
        total = total + lengths_ref[0, p]
        slot = places_ref[adapters_ref[0, p]]
        inside = (column >= start) & (column < total)
        slots.append(slot)
        members.append(inside.astype(F32))
        owned = owned + jnp.where(inside, jnp.where(slot == me, 1.0, 0.0), 0.0)
        first = jnp.where(inside, start, first)
        slot_lane = jnp.where(lane // ranks == p, slot, slot_lane)

    adapter_row = lax.broadcasted_iota(jnp.int32, (adapters, 128), 0)
    out_factor = jnp.zeros((CHUNK, 128), F32)
    down_factor = jnp.zeros((CHUNK, 128), F32)
    for r in range(ranks):
        pick = ((adapter_row == slot_lane) & (lax.rem(lane, ranks) == r)).astype(BF16)
        out_factor = out_factor + dot(bo_ref[r], pick)
        down_factor = down_factor + dot(bd_ref[r], pick)
    diagonal = lax.broadcasted_iota(jnp.int32, (CHUNK, CHUNK), 0) == lax.broadcasted_iota(
        jnp.int32, (CHUNK, CHUNK), 1
    )
    gain = jnp.sum(jnp.where(diagonal, gain_ref[...].astype(F32), 0.0), axis=1, keepdims=True)
    gain_lane = prompts * ranks
    out_factor = jnp.where(lane == gain_lane, gain, out_factor)
    factors[c, y, x] = jnp.concatenate([out_factor, down_factor], axis=1).astype(BF16)

    pl.semaphore_wait(barrier, len(peers))

    places = [mod(z + k, zs) for k in range(zs)]
    wo_pairs = [sems.take() for _ in range(zs - 1)]
    for k in range(1, zs):
        launch(lambda k=k: copy(wo_all.at[z], wo_all.at[z], wo_pairs[k - 1], to_z(k)))
    ups, downs = zs // 2, (zs - 1) // 2
    z_pairs = {}
    for way, hops in ((1, ups), (-1, downs)):
        for hop in range(1, hops + 1):
            z_pairs[way, hop] = (sems.take(), sems.take())

    def z_slot(way, hop):
        return mod(z - way * hop, zs)

    def z_block(way, hop):
        slot = z_slot(way, hop)
        return (
            gu_all.at[slot],
            down_all.at[pl.ds(pl.multiple_of(slot * down_cols, down_cols), down_cols), :],
        )

    def z_wait(hop):
        for way, hops in ((1, ups), (-1, downs)):
            if 1 <= hop <= hops:
                for n, block in enumerate(z_block(way, hop)):
                    arrived(block, z_pairs[way, hop][n])

    def z_step(hop):
        z_wait(hop - 1)
        for way, hops in ((1, ups), (-1, downs)):
            if hop <= hops:
                for n in range(2):

                    def make(way=way, n=n):
                        block = z_block(way, hop - 1)[n]
                        return copy(block, block, z_pairs[way, hop][n], to_z(way))

                    launch(make)

    factor_y = [None] + [sems.take() for _ in range(1, ys)]
    factor_x = {(r, k): sems.take() for r in range(ys) for k in range(1, xs)}
    factor_pair = [sems.take() for _ in range(ys)]
    near_first = sorted(range(ys), key=lambda k: min(k, ys - k))

    def factor_send():
        for k in near_first[1:]:
            launch(lambda k=k: copy(factors.at[c, y, x], factors.at[c, y, x], factor_y[k], to_y(k)))

    def factor_cross():
        for r in near_first:
            if r > 0:
                arrived(factors.at[c, mod(y - r, ys), x], factor_y[r])
            for k in range(1, xs):

                def make(r=r, k=k):
                    block = factors.at[c, mod(y - r, ys), x]
                    return copy(block, block, factor_x[r, k], to_x(k))

                launch(make)

    def factor_share():
        for r in near_first:
            for k in range(1, xs):
                arrived(factors.at[c, mod(y - r, ys), mod(x - k, xs)], factor_x[r, k])

            def make(r=r):
                block = factors.at[c, mod(y - r, ys)]
                return copy(block, block, factor_pair[r], partner())

            launch(make)

    def factor_wait():
        for r in near_first:
            arrived(factors.at[1 - c, mod(y - r, ys)], factor_pair[r])

    factor_send()
    z_step(1)

    for n in range(2 * kv_heads):
        loads[n].wait()
    for n in range(kv_heads):
        values_all[n] = kv_all[kv_heads + n].astype(F32).T.astype(BF16)

    def attend(h, carry):
        kv = h // group
        for block in range(2):
            lo, hi = block * half, (block + 1) * half
            scores = lax.dot_general(
                kv_all[kv, :hi, :],
                q_all[h, lo:hi, :],
                (((1,), (1,)), ((), ())),
                preferred_element_type=F32,
            )
            row = lax.broadcasted_iota(jnp.int32, (hi, half), 0)
            allowed = (row >= first[:, lo:hi]) & (row <= column[:, lo:hi])
            scores = jnp.where(allowed, scores * HEAD ** (-0.5), -1e30)
            top = jnp.max(scores, axis=0, keepdims=True)
            weights = jnp.exp(scores - top)
            total = jnp.sum(weights, axis=0, keepdims=True)
            mixed = dot(values_all[kv, :, :hi], weights.astype(BF16))
            attn_all[pl.ds(pl.multiple_of(h * HEAD, HEAD), HEAD), lo:hi] = (mixed / total).astype(BF16)
        return carry

    def attend_heads(lo, hi):
        for h in range(lo, hi):
            loads[2 * kv_heads + h].wait()
        lax.fori_loop(lo, hi, attend, 0)

    cut_one, cut_two = (heads * 3) // 8, (heads * 6) // 8
    attend_heads(0, cut_one)
    factor_cross()
    attend_heads(cut_one, cut_two)
    z_step(2)
    factor_share()
    attend_heads(cut_two, heads)

    class AllReduce:
        def __init__(self, pair_buf, x_buf, xin, yin, back):
            self.bufs = (pair_buf, x_buf, xin, yin, back)
            self.pairs = [sems.take() for _ in range(2 + (xs - 1) + (ys - 1))]
            self.kind = pair_buf.dtype

        def start(self, value):
            pair_buf = self.bufs[0]
            pair_buf[0] = value[:, :half].astype(self.kind)
            pair_buf[1] = value[:, half:].astype(self.kind)
            launch(lambda: copy(pair_buf.at[1 - c], pair_buf.at[2], self.pairs[0], partner()))

        def cross(self):
            pair_buf, x_buf, xin, yin, back = self.bufs
            arrived(pair_buf.at[2], self.pairs[0])
            x_buf[0] = (pair_buf[c].astype(F32) + pair_buf[2].astype(F32)).astype(self.kind)
            for k in range(1, xs):
                launch(lambda k=k: copy(x_buf.at[0], xin.at[k - 1], self.pairs[k], to_x(k)))

        def along(self):
            pair_buf, x_buf, xin, yin, back = self.bufs
            total = x_buf[0].astype(F32)
            for k in range(1, xs):
                arrived(xin.at[k - 1], self.pairs[k])
                total = total + xin[k - 1].astype(F32)
            x_buf[1] = total.astype(self.kind)
            for k in range(1, ys):
                launch(
                    lambda k=k: copy(x_buf.at[1], yin.at[k - 1], self.pairs[xs - 1 + k], to_y(k))
                )

        def share(self):
            pair_buf, x_buf, xin, yin, back = self.bufs
            total = x_buf[1].astype(F32)
            for k in range(1, ys):
                arrived(yin.at[k - 1], self.pairs[xs - 1 + k])
                total = total + yin[k - 1].astype(F32)
            back[c] = total.astype(self.kind)
            launch(lambda: copy(back.at[c], back.at[c], self.pairs[-1], partner()))

        def result(self):
            back = self.bufs[4]
            arrived(back.at[1 - c], self.pairs[-1])
            return jnp.concatenate([back[0], back[1]], axis=1).astype(F32)

    def expand(rank):
        return jnp.concatenate([rank * members[p] for p in range(prompts)], axis=0).astype(BF16)

    def padded(rows, full):
        return jnp.concatenate([rows, jnp.zeros((full - rows.shape[0], tokens), BF16)], axis=0)

    out_reduce = AllReduce(rank_pair, rank_x, rank_xin, rank_yin, rank_back)
    gu_reduce = AllReduce(gu_pair, gu_x, gu_xin, gu_yin, gu_back)
    attn = attn_all[...]
    out_reduce.start(dot(ao_ref[...], attn) * owned)
    for k in range(1, zs):
        arrived(wo_all.at[places[zs - k]], wo_pairs[k - 1])
    weights = jnp.concatenate([wo_all[k] for k in range(zs)], axis=1)
    base = residual_ref[...].astype(F32) + dot(weights, attn)
    middle_ref[...] = base
    gathered[c, y, x] = base.astype(BF16)
    out_reduce.cross()

    def hops_of(way, j):
        long = (way == 1) == (j < (xs + 1) // 2)
        return ys // 2 if long else (ys - 1) // 2

    most = ys // 2
    ring_keys = [
        (way, hop, j)
        for j in range(xs)
        for way in (1, -1)
        for hop in range(1, hops_of(way, j) + 1)
    ]
    ring_slot = {key: n for n, key in enumerate(ring_keys)}
    branch_copies = max(xs - 1 + len(ring_keys), ys - 1 + ys * (xs - 1))
    row_pairs = [sems.take() for _ in range(ys)]
    gather_sems = sems.reserve(branch_copies)

    def beside_gather():
        z_step(3)
        out_reduce.along()

    def branch(run):
        kept = len(pending)
        run()
        made = pending[kept:]
        del pending[kept:]
        return made

    beside = []

    def gather_zero():
        sems = gather_sems.again()
        own = gathered.at[0, y, x]
        x_pairs = [None] + [sems.take() for _ in range(1, xs)]
        ring = {key: sems.take() for key in ring_keys}
        sent = []
        for k in range(1, xs):
            sent.append(send(own, own, x_pairs[k], to_x(k)))
        shared = []
        for hop in range(1, most + 2):
            for j in range(xs):
                xj = mod(x - j, xs)
                if hop == 1 and j > 0:
                    arrived(gathered.at[0, y, xj], x_pairs[j])
                for way in (1, -1):
                    hops = hops_of(way, j)
                    block = gathered.at[0, mod(y - way * (hop - 1), ys), xj]
                    if 1 < hop <= hops + 1:
                        arrived(block, ring[way, hop - 1, j])
                    if hop <= hops:
                        sent.append(send(block, block, ring[way, hop, j], to_y(way)))
            if hop == 1:
                beside.append(branch(beside_gather))
            for k in ((hop - 1) % ys, (1 - hop) % ys):
                if k not in shared:
                    shared.append(k)
                    if k != ys // 2 or hop == most + 1:
                        block = gathered.at[0, mod(y - k, ys)]
                        sent.append(send(block, block, row_pairs[k], partner()))
        for made in sent:
            made.wait_send()

    def gather_one():
        sems = gather_sems.again()
        own = gathered.at[1, y, x]
        y_pairs = [None] + [sems.take() for _ in range(1, ys)]
        x_pairs = {(r, k): sems.take() for r in range(ys) for k in range(1, xs)}
        sent = []
        for k in near_first[1:]:
            sent.append(send(own, own, y_pairs[k], to_y(k)))
        for r in near_first:
            block = gathered.at[1, mod(y - r, ys), x]
            if r > 0:
                arrived(block, y_pairs[r])
            for k in range(1, xs):
                sent.append(send(block, block, x_pairs[r, k], to_x(k)))
            if r == 0:
                branch(beside_gather)
        for r in near_first:
            for k in range(1, xs):
                arrived(gathered.at[1, mod(y - r, ys), mod(x - k, xs)], x_pairs[r, k])
            block = gathered.at[1, mod(y - r, ys)]
            sent.append(send(block, block, row_pairs[r], partner()))
        for made in sent:
            made.wait_send()

    pl.when(c == 0)(gather_zero)
    pl.when(c == 1)(gather_one)
    pending.extend(beside[0])
    out_reduce.share()
    factor_wait()
    for k in near_first:
        arrived(gathered.at[1 - c, mod(y - k, ys)], row_pairs[k])
    z_step(4)

    out_rank = padded(expand(ADAPTER_SCALE * out_reduce.result()), 128)
    middle_ref[...] += dot(factors[c, y, x, :, :128], out_rank)
    per_row = width // ys
    squares = jnp.zeros((8, tokens), F32)
    for row in range(ys):
        for core in range(CORES):
            block = factors[core, row].reshape(xs * CHUNK, 256)[:, :128]
            full = gathered[core, row].reshape(xs * CHUNK, tokens).astype(F32) + dot(block, out_rank)
            squares = squares + jnp.sum((full * full).reshape(-1, 8, tokens), axis=0)
            scaled = (full * block[:, gain_lane : gain_lane + 1].astype(F32)).astype(BF16)
            for col in range(xs):
                top = row * per_row + (col * CORES + core) * CHUNK
                normed[top : top + CHUNK, :] = scaled[col * CHUNK : (col + 1) * CHUNK]
    squares = jnp.sum(squares, axis=0, keepdims=True)
    inverse = lax.rsqrt(squares / width + EPS)

    gu_reduce.start(dot(agu_ref[...], normed[...]) * (owned * inverse))
    for hop in range(5, most + 1):
        z_step(hop)
    gu_reduce.cross()
    z_wait(max(ups, downs))
    weights = jnp.concatenate([gu_all[k] for k in range(zs)], axis=1)
    gu_reduce.along()
    joint = dot(weights, normed[...]) * inverse
    gu_reduce.share()
    gu_rank = gu_reduce.result()

    def hidden_correction(which, rank):
        rows = jnp.concatenate([bgu_ref[which, slot] for slot in slots], axis=0)
        return ADAPTER_SCALE * dot(rows.astype(F32).T.astype(BF16), expand(rank))

    gate = joint[:hidden] + hidden_correction(0, gu_rank[:ranks])
    up = joint[hidden:] + hidden_correction(1, gu_rank[ranks:])
    hidden_state = (jax.nn.gelu(gate, approximate=True) * up).astype(BF16)

    a_rows = jnp.concatenate([ad_ref[slot] for slot in slots], axis=0)
    shares = ADAPTER_SCALE * dot(a_rows, hidden_state)
    down_rank = jnp.concatenate(
        [shares[p * ranks : (p + 1) * ranks] * members[p] for p in range(prompts)], axis=0
    ).astype(BF16)
    source = jnp.concatenate([hidden_state, padded(down_rank, 128)], axis=0)
    far_first = near_first[::-1]
    share_pairs = [sems.take() for _ in range(ys)]
    scatter_sems = sems.reserve(branch_copies)
    for r in far_first:
        row = mod(y + r, ys)
        weights = down_all[pl.ds(pl.multiple_of(row * per_row, per_row), per_row), :]
        extra = jnp.concatenate(
            [factors[core, row, col, :, 128:] for col in range(xs) for core in range(CORES)], axis=0
        )
        block = dot(jnp.concatenate([weights, extra], axis=1), source).astype(BF16)
        for col in range(xs):
            for core in range(CORES):
                top = (col * CORES + core) * CHUNK
                partial[core, r, col] = block[top : top + CHUNK]
        launch(
            lambda r=r: copy(partial.at[1 - c, r], pair_in.at[r], share_pairs[r], partner())
        )

    def add_pair(r):
        arrived(pair_in.at[r], share_pairs[r])
        summed[r] = (partial[c, r].astype(F32) + pair_in[r].astype(F32)).astype(BF16)

    def scatter_zero():
        sems = scatter_sems.again()
        ring = {key: sems.take() for key in ring_keys}
        x_pairs = [None] + [sems.take() for _ in range(1, xs)]
        sent, added = [], []
        for hop in range(1, most + 1):
            todo = []
            for j in range(xs):
                for way in (1, -1):
                    hops = hops_of(way, j)
                    if hop <= hops:
                        todo.append((j, way, (way * (hops + 1 - hop)) % ys))
            if hop == 1:
                todo.sort(key=lambda item: far_first.index(item[2]))
            for j, way, r in todo:
                if r not in added:
                    add_pair(r)
                    added.append(r)
                n = ring_slot[way, hop, j]
                if hop == 1:
                    block = summed.at[r, j]
                else:
                    before = ring_slot[way, hop - 1, j]
                    arrived(ring_in.at[before], ring[way, hop - 1, j])
                    total = summed[r, j].astype(F32) + ring_in[before].astype(F32)
                    ring_out[n] = total.astype(BF16)
                    block = ring_out.at[n]
                sent.append(send(block, ring_in.at[n], ring[way, hop, j], to_y(way)))
            if hop == 1:
                for r in far_first:
                    if r not in added:
                        add_pair(r)
                        added.append(r)
        for j in range(xs):
            total = summed[0, j].astype(F32)
            for way in (1, -1):
                hops = hops_of(way, j)
                if hops > 0:
                    n = ring_slot[way, hops, j]
                    arrived(ring_in.at[n], ring[way, hops, j])
                    total = total + ring_in[n].astype(F32)
            last_out[j] = total.astype(BF16)
        for k in range(1, xs):
            sent.append(send(last_out.at[mod(x + k, xs)], last_in.at[k], x_pairs[k], to_x(k)))
        total = last_out[x].astype(F32)
        for k in range(1, xs):
            arrived(last_in.at[k], x_pairs[k])
            total = total + last_in[k].astype(F32)
        middle_ref[...] = middle_ref[...].astype(BF16).astype(F32) + total
        for made in sent:
            made.wait_send()

    def scatter_one():
        sems = scatter_sems.again()
        x_pairs = {(r, k): sems.take() for r in range(ys) for k in range(1, xs)}
        y_pairs = [None] + [sems.take() for _ in range(1, ys)]
        sent = []
        for r in far_first:
            add_pair(r)
            for k in range(1, xs):
                sent.append(
                    send(summed.at[r, mod(x + k, xs)], cross_in.at[r, k - 1], x_pairs[r, k], to_x(k))
                )
        for r in far_first:
            total = summed[r, x].astype(F32)
            for k in range(1, xs):
                arrived(cross_in.at[r, k - 1], x_pairs[r, k])
                total = total + cross_in[r, k - 1].astype(F32)
            last_out[r] = total.astype(BF16)
            if r > 0:
                sent.append(send(last_out.at[r], last_in.at[r], y_pairs[r], to_y(r)))
        total = last_out[0].astype(F32)
        for r in range(1, ys):
            arrived(last_in.at[r], y_pairs[r])
            total = total + last_in[r].astype(F32)
        middle_ref[...] = middle_ref[...].astype(BF16).astype(F32) + total
        for made in sent:
            made.wait_send()

    pl.when(c == 0)(scatter_zero)
    pl.when(c == 1)(scatter_one)
    out_ref[...] = middle_ref[...].astype(BF16)
    for make in pending:
        make().wait_send()


def main_call(dims, args):
    zs, ys, xs = dims
    tokens, width = args[3].shape
    heads = width // HEAD
    kv_heads = args[4].shape[1] // (2 * HEAD)
    half = tokens // 2
    gate = args[10]
    hidden = gate.shape[1]
    span = gate.shape[0]
    ranks = args[8].shape[0]
    rings = xs * (ys - 1)

    def reduce_buffers(rows, kind):
        return [
            pltpu.VMEM((3, rows, half), kind),
            pltpu.VMEM((2, rows, half), kind),
            pltpu.VMEM((xs - 1, rows, half), kind),
            pltpu.VMEM((ys - 1, rows, half), kind),
            pltpu.VMEM((2, rows, half), kind),
        ]

    scratch = [
        pltpu.VMEM((heads, tokens, HEAD), BF16),
        pltpu.VMEM((2 * kv_heads, tokens, HEAD), BF16),
        pltpu.VMEM((kv_heads, HEAD, tokens), BF16),
        pltpu.VMEM((width, tokens), BF16),
        pltpu.VMEM((zs, CHUNK, span), BF16),
        pltpu.VMEM((zs, 2 * hidden, span), BF16),
        pltpu.VMEM((width, hidden), BF16),
        pltpu.VMEM((CORES, ys, xs, CHUNK, 256), BF16),
        pltpu.VMEM((CHUNK, tokens), F32),
        pltpu.VMEM((CORES, ys, xs, CHUNK, tokens), BF16),
        pltpu.VMEM((width, tokens), BF16),
        pltpu.VMEM((CORES, ys, xs, CHUNK, tokens), BF16),
        pltpu.VMEM((ys, xs, CHUNK, tokens), BF16),
        pltpu.VMEM((ys, xs, CHUNK, tokens), BF16),
        pltpu.VMEM((rings, CHUNK, tokens), BF16),
        pltpu.VMEM((rings, CHUNK, tokens), BF16),
        pltpu.VMEM((ys, xs - 1, CHUNK, tokens), BF16),
        pltpu.VMEM((max(xs, ys), CHUNK, tokens), BF16),
        pltpu.VMEM((max(xs, ys), CHUNK, tokens), BF16),
    ]
    scratch += reduce_buffers(ranks, BF16)
    scratch += reduce_buffers(2 * ranks, BF16)
    scratch += [
        pltpu.SemaphoreType.DMA((heads + 2 * kv_heads,)),
        pltpu.SemaphoreType.DMA((SEMAPHORES,)),
        pltpu.SemaphoreType.DMA((SEMAPHORES,)),
    ]
    smem = pl.BlockSpec(memory_space=pltpu.SMEM)
    vmem = pl.BlockSpec(memory_space=pltpu.VMEM)
    hbm = pl.BlockSpec(memory_space=pl.ANY)
    return pl.pallas_call(
        functools.partial(main_kernel, dims),
        out_shape=jax.ShapeDtypeStruct((CHUNK, tokens), BF16),
        in_specs=[smem] * 3 + [hbm] * 2 + [vmem] * (len(args) - 5),
        out_specs=vmem,
        scratch_shapes=scratch,
        compiler_params=pltpu.CompilerParams(
            collective_id=0, has_side_effects=True, vmem_limit_bytes=60 * 1024 * 1024
        ),
    )(*args)


def body(
    dims,
    residual_input,
    queries,
    key_value_pairs,
    prompt_length_list,
    prompt_adapter_index,
    adapter_position,
    output_matrix,
    output_factor_first,
    output_factor_second,
    norm_weight,
    gate_up_matrix,
    gate_up_factor_first,
    gate_up_factor_second,
    down_matrix,
    down_factor_first,
    down_factor_second,
):
    args = [
        prompt_length_list,
        prompt_adapter_index,
        adapter_position,
        queries,
        key_value_pairs,
        residual_input.T,
        norm_weight.reshape(1, -1),
        output_matrix.T,
        output_factor_first[0].T,
        output_factor_second.transpose(1, 2, 0),
        gate_up_matrix[:, 0, :],
        gate_up_matrix[:, 1, :],
        gate_up_factor_first[0].T,
        gate_up_factor_second,
        down_matrix,
        down_factor_first.transpose(1, 2, 0),
        down_factor_second.transpose(1, 2, 0),
    ]
    return main_call(dims, args).T


def solution(mesh):
    placed = (
        P("req", "hid"),
        P("req", None),
        P("req", None),
        P("req", None),
        P("req", None),
        P(),
        P("req", "hid"),
        P("hid", None, None),
        P(None, None, "hid"),
        P("hid"),
        P("req", None, "hid"),
        P("hid", None, None),
        P(None, None, None, "hid"),
        P("hid", "req"),
        P("hid", None, None),
        P(None, None, "hid"),
    )
    dims = (mesh.shape["req"], mesh.shape["hid"] // (CORES * GRID_X), GRID_X)
    return jax.shard_map(
        functools.partial(body, dims),
        mesh=mesh,
        in_specs=placed,
        out_specs=P("req", "hid"),
        check_vma=False,
    )
```

time: 121 us -> 97.4 us (0.80)
  the two profiles are of different devices: /device:TPU:1 before, /device:TPU:16 now
where the time goes in v2:
time: 97.4 us; the launch traced here: 97.2 us
  Pallas kernels  94 us (97%)
  local copies, waits for them, and re-layouts  3.23 us (3%)
    pallas_call x1, Pallas kernels, main_call(): pl.pallas_call(functools.partial(main_kernel, dims), out_shape=jax.ShapeD...  94 us

profile of v2, /device:TPU:16, one launch (start us, length us, event | category | flops | bytes accessed | tf_op | source)
XLA Modules:
  0.0 97.2 jit_solution(4822855146259378390)
XLA Ops:
  0.0 1.2 %fusion = (bf16[256,1,128]{2,1,0:T(2,128)(2,1)S(1)}, bf16[256,1,128]{2,1,0:T(2,128)(2,1)S(1)}) fusion(bf16[256,2,128]{2,1,0:T(2,128)(2,1)} %param.26), kind=kLoop, calls=%fused_computation.2 | loop fusion | bytes 262144 | tf_op jit(solution)/shard_map/slice | solution.py:753
  1.2 0.7 copy_bitcast_fusion
  1.9 94.0 %shard_map.154 = bf16[32,512]{1,0:T(8,128)(2,1)} custom-call(s32[1,6]{1,0:T(1,128)} %lengths_ref.1, s32[1,6]{1,0:T(1,128)} %adapters_ref.1, s32[64]{0:T(128)} %places_ref.1, bf16[512,2048]{1,0:T(8,128)(2,1)} %queries_ref.1, bf16[512,1024]{1,0:T(8,128)(2,1)} %pairs_ref.1, bf16[32,512]{1,0:T(8,128)(2,1)} %bitcast.23, bf16[1,32]{1,0:T(2,128)(2,1)} %bitcast.25, ...), custom_call_target="tpu_custom_call" | custom-call | tf_op jit(solution)/shard_map/pallas_call | solution.py:710
  95.8 1.4 %copy.24 = bf16[512,32]{0,1:T(8,128)(2,1)} copy(bf16[512,32]{0,1:T(8,128)(2,1)} %bitcast.18) | data formatting | bytes 65536

commit v3 on v2

--- a/solution.py
+++ b/solution.py
@@ -67,14 +67,17 @@
     wo_ref,
     ao_ref,
     bo_ref,
-    gate_ref,
-    up_ref,
+    gate_up_ref,
+    agu_hbm,
+    bgu_hbm,
+    down_ref,
+    ad_hbm,
+    bd_ref,
+    out_ref,
     agu_ref,
     bgu_ref,
-    down_ref,
     ad_ref,
-    bd_ref,
-    out_ref,
+    bias_all,
     q_all,
     kv_all,
     values_all,
@@ -179,6 +182,8 @@
                 local_sems.at[2 * kv_heads + h],
             )
         )
+    for n, (src, dst) in enumerate(((agu_hbm, agu_ref), (bgu_hbm, bgu_ref), (ad_hbm, ad_ref))):
+        loads.append(pltpu.make_async_copy(src, dst, local_sems.at[2 * kv_heads + heads + n]))
     for load in loads:
         load.start()
 
@@ -191,10 +196,11 @@
         pl.semaphore_signal(barrier, inc=1, device_id=peer, device_id_type=MESH)
 
     wo_all[z] = wo_ref[...]
-    hidden = gate_ref.shape[1]
+    hidden = gate_up_ref.shape[2]
     down_cols = down_ref.shape[1]
-    gu_all[z, 0:hidden, :] = gate_ref[...].astype(F32).T.astype(BF16)
-    gu_all[z, hidden : 2 * hidden, :] = up_ref[...].astype(F32).T.astype(BF16)
+    both = gate_up_ref[...].astype(F32)
+    for n in range(2):
+        gu_all[z, n * hidden : (n + 1) * hidden, :] = both[:, n, :].T.astype(BF16)
     down_rows = pl.ds(pl.multiple_of(z * down_cols, down_cols), down_cols)
     down_all[down_rows, :] = down_ref[...].astype(F32).T.astype(BF16)
 
@@ -217,6 +223,83 @@
         first = jnp.where(inside, start, first)
         slot_lane = jnp.where(lane // ranks == p, slot, slot_lane)
 
+    pl.semaphore_wait(barrier, len(peers))
+
+    places = [mod(z + k, zs) for k in range(zs)]
+    wo_pairs = [sems.take() for _ in range(zs - 1)]
+    for k in range(1, zs):
+        launch(lambda k=k: copy(wo_all.at[z], wo_all.at[z], wo_pairs[k - 1], to_z(k)))
+    ups, downs = zs // 2, (zs - 1) // 2
+    z_pairs = {}
+    for way, hops in ((1, ups), (-1, downs)):
+        for hop in range(1, hops + 1):
+            z_pairs[way, hop] = (sems.take(), sems.take())
+
+    def z_slot(way, hop):
+        return mod(z - way * hop, zs)
+
+    def z_block(way, hop):
+        slot = z_slot(way, hop)
+        return (
+            gu_all.at[slot],
+            down_all.at[pl.ds(pl.multiple_of(slot * down_cols, down_cols), down_cols), :],
+        )
+
+    def z_wait(hop):
+        for way, hops in ((1, ups), (-1, downs)):
+            if 1 <= hop <= hops:
+                for n, block in enumerate(z_block(way, hop)):
+                    arrived(block, z_pairs[way, hop][n])
+
+    def z_step(hop):
+        z_wait(hop - 1)
+        for way, hops in ((1, ups), (-1, downs)):
+            if hop <= hops:
+                for n in range(2):
+
+                    def make(way=way, n=n):
+                        block = z_block(way, hop - 1)[n]
+                        return copy(block, block, z_pairs[way, hop][n], to_z(way))
+
+                    launch(make)
+
+    factor_y = [None] + [sems.take() for _ in range(1, ys)]
+    factor_x = {(r, k): sems.take() for r in range(ys) for k in range(1, xs)}
+    factor_pair = [sems.take() for _ in range(ys)]
+    near_first = sorted(range(ys), key=lambda k: min(k, ys - k))
+
+    def factor_send():
+        for k in near_first[1:]:
+            launch(lambda k=k: copy(factors.at[c, y, x], factors.at[c, y, x], factor_y[k], to_y(k)))
+
+    def factor_cross():
+        for r in near_first:
+            if r > 0:
+                arrived(factors.at[c, mod(y - r, ys), x], factor_y[r])
+            for k in range(1, xs):
+
+                def make(r=r, k=k):
+                    block = factors.at[c, mod(y - r, ys), x]
+                    return copy(block, block, factor_x[r, k], to_x(k))
+
+                launch(make)
+
+    def factor_share():
+        for r in near_first:
+            for k in range(1, xs):
+                arrived(factors.at[c, mod(y - r, ys), mod(x - k, xs)], factor_x[r, k])
+
+            def make(r=r):
+                block = factors.at[c, mod(y - r, ys)]
+                return copy(block, block, factor_pair[r], partner())
+
+            launch(make)
+
+    def factor_wait():
+        for r in near_first:
+            arrived(factors.at[1 - c, mod(y - r, ys)], factor_pair[r])
+
+    z_step(1)
     adapter_row = lax.broadcasted_iota(jnp.int32, (adapters, 128), 0)
     out_factor = jnp.zeros((CHUNK, 128), F32)
     down_factor = jnp.zeros((CHUNK, 128), F32)
@@ -231,92 +314,17 @@
     gain_lane = prompts * ranks
     out_factor = jnp.where(lane == gain_lane, gain, out_factor)
     factors[c, y, x] = jnp.concatenate([out_factor, down_factor], axis=1).astype(BF16)
-
-    pl.semaphore_wait(barrier, len(peers))
-
-    places = [mod(z + k, zs) for k in range(zs)]
-    wo_pairs = [sems.take() for _ in range(zs - 1)]
-    for k in range(1, zs):
-        launch(lambda k=k: copy(wo_all.at[z], wo_all.at[z], wo_pairs[k - 1], to_z(k)))
-    ups, downs = zs // 2, (zs - 1) // 2
-    z_pairs = {}
-    for way, hops in ((1, ups), (-1, downs)):
-        for hop in range(1, hops + 1):
-            z_pairs[way, hop] = (sems.take(), sems.take())
-
-    def z_slot(way, hop):
-        return mod(z - way * hop, zs)
-
-    def z_block(way, hop):
-        slot = z_slot(way, hop)
-        return (
-            gu_all.at[slot],
-            down_all.at[pl.ds(pl.multiple_of(slot * down_cols, down_cols), down_cols), :],
-        )
-
-    def z_wait(hop):
-        for way, hops in ((1, ups), (-1, downs)):
-            if 1 <= hop <= hops:
-                for n, block in enumerate(z_block(way, hop)):
-                    arrived(block, z_pairs[way, hop][n])
-
-    def z_step(hop):
-        z_wait(hop - 1)
-        for way, hops in ((1, ups), (-1, downs)):
-            if hop <= hops:
-                for n in range(2):
-
-                    def make(way=way, n=n):
-                        block = z_block(way, hop - 1)[n]
-                        return copy(block, block, z_pairs[way, hop][n], to_z(way))
-
-                    launch(make)
-
-    factor_y = [None] + [sems.take() for _ in range(1, ys)]
-    factor_x = {(r, k): sems.take() for r in range(ys) for k in range(1, xs)}
-    factor_pair = [sems.take() for _ in range(ys)]
-    near_first = sorted(range(ys), key=lambda k: min(k, ys - k))
-
-    def factor_send():
-        for k in near_first[1:]:
-            launch(lambda k=k: copy(factors.at[c, y, x], factors.at[c, y, x], factor_y[k], to_y(k)))
-
-    def factor_cross():
-        for r in near_first:
-            if r > 0:
-                arrived(factors.at[c, mod(y - r, ys), x], factor_y[r])
-            for k in range(1, xs):
-
-                def make(r=r, k=k):
-                    block = factors.at[c, mod(y - r, ys), x]
-                    return copy(block, block, factor_x[r, k], to_x(k))
-
-                launch(make)
-
-    def factor_share():
-        for r in near_first:
-            for k in range(1, xs):
-                arrived(factors.at[c, mod(y - r, ys), mod(x - k, xs)], factor_x[r, k])
-
-            def make(r=r):
-                block = factors.at[c, mod(y - r, ys)]
-                return copy(block, block, factor_pair[r], partner())
-
-            launch(make)
-
-    def factor_wait():
-        for r in near_first:
-            arrived(factors.at[1 - c, mod(y - r, ys)], factor_pair[r])
-
     factor_send()
-    z_step(1)
 
     for n in range(2 * kv_heads):
         loads[n].wait()
     for n in range(kv_heads):
         values_all[n] = kv_all[kv_heads + n].astype(F32).T.astype(BF16)
 
-    def attend(h, carry):
+    row = lax.broadcasted_iota(jnp.int32, (tokens, tokens), 0)
+    bias_all[...] = jnp.where((row >= first) & (row <= column), 0.0, -1e30)
+
+    def attend_one(h):
         kv = h // group
         for block in range(2):
             lo, hi = block * half, (block + 1) * half
@@ -326,28 +334,28 @@
                 (((1,), (1,)), ((), ())),
                 preferred_element_type=F32,
             )
-            row = lax.broadcasted_iota(jnp.int32, (hi, half), 0)
-            allowed = (row >= first[:, lo:hi]) & (row <= column[:, lo:hi])
-            scores = jnp.where(allowed, scores * HEAD ** (-0.5), -1e30)
+            scores = scores * HEAD ** (-0.5) + bias_all[:hi, lo:hi]
             top = jnp.max(scores, axis=0, keepdims=True)
             weights = jnp.exp(scores - top)
             total = jnp.sum(weights, axis=0, keepdims=True)
             mixed = dot(values_all[kv, :, :hi], weights.astype(BF16))
             attn_all[pl.ds(pl.multiple_of(h * HEAD, HEAD), HEAD), lo:hi] = (mixed / total).astype(BF16)
+
+    def attend(n, carry):
+        attend_one(2 * n)
+        attend_one(2 * n + 1)
         return carry
 
     def attend_heads(lo, hi):
         for h in range(lo, hi):
             loads[2 * kv_heads + h].wait()
-        lax.fori_loop(lo, hi, attend, 0)
-
-    cut_one, cut_two = (heads * 3) // 8, (heads * 6) // 8
-    attend_heads(0, cut_one)
+        lax.fori_loop(lo // 2, hi // 2, attend, 0)
+
+    cut = 2 * ((heads * 3) // 8)
+    attend_heads(0, cut)
+    z_step(2)
     factor_cross()
-    attend_heads(cut_one, cut_two)
-    z_step(2)
-    factor_share()
-    attend_heads(cut_two, heads)
+    attend_heads(cut, heads)
 
     class AllReduce:
         def __init__(self, pair_buf, x_buf, xin, yin, back):
@@ -429,8 +437,12 @@
     gather_sems = sems.reserve(branch_copies)
 
     def beside_gather():
+        out_reduce.along()
+        factor_share()
         z_step(3)
-        out_reduce.along()
+
+    def late_gather():
+        z_step(4)
 
     def branch(run):
         kept = len(pending)
@@ -464,6 +476,8 @@
                         sent.append(send(block, block, ring[way, hop, j], to_y(way)))
             if hop == 1:
                 beside.append(branch(beside_gather))
+            if hop == most:
+                beside.append(branch(late_gather))
             for k in ((hop - 1) % ys, (1 - hop) % ys):
                 if k not in shared:
                     shared.append(k)
@@ -489,7 +503,9 @@
                 sent.append(send(block, block, x_pairs[r, k], to_x(k)))
             if r == 0:
                 branch(beside_gather)
-        for r in near_first:
+        for n, r in enumerate(near_first):
+            if n == ys // 2:
+                branch(late_gather)
             for k in range(1, xs):
                 arrived(gathered.at[1, mod(y - r, ys), mod(x - k, xs)], x_pairs[r, k])
             block = gathered.at[1, mod(y - r, ys)]
@@ -499,12 +515,11 @@
 
     pl.when(c == 0)(gather_zero)
     pl.when(c == 1)(gather_one)
-    pending.extend(beside[0])
+    pending.extend(beside[0] + beside[1])
     out_reduce.share()
     factor_wait()
     for k in near_first:
         arrived(gathered.at[1 - c, mod(y - k, ys)], row_pairs[k])
-    z_step(4)
 
     out_rank = padded(expand(ADAPTER_SCALE * out_reduce.result()), 128)
     middle_ref[...] += dot(factors[c, y, x, :, :128], out_rank)
@@ -522,6 +537,8 @@
     squares = jnp.sum(squares, axis=0, keepdims=True)
     inverse = lax.rsqrt(squares / width + EPS)
 
+    for load in loads[2 * kv_heads + heads :]:
+        load.wait()
     gu_reduce.start(dot(agu_ref[...], normed[...]) * (owned * inverse))
     for hop in range(5, most + 1):
         z_step(hop)
@@ -661,9 +678,7 @@
     heads = width // HEAD
     kv_heads = args[4].shape[1] // (2 * HEAD)
     half = tokens // 2
-    gate = args[10]
-    hidden = gate.shape[1]
-    span = gate.shape[0]
+    span, _, hidden = args[10].shape
     ranks = args[8].shape[0]
     rings = xs * (ys - 1)
 
@@ -677,6 +692,10 @@
         ]
 
     scratch = [
+        pltpu.VMEM(args[11].shape, BF16),
+        pltpu.VMEM(args[12].shape, BF16),
+        pltpu.VMEM(args[14].shape, BF16),
+        pltpu.VMEM((tokens, tokens), F32),
         pltpu.VMEM((heads, tokens, HEAD), BF16),
         pltpu.VMEM((2 * kv_heads, tokens, HEAD), BF16),
         pltpu.VMEM((kv_heads, HEAD, tokens), BF16),
@@ -700,7 +719,7 @@
     scratch += reduce_buffers(ranks, BF16)
     scratch += reduce_buffers(2 * ranks, BF16)
     scratch += [
-        pltpu.SemaphoreType.DMA((heads + 2 * kv_heads,)),
+        pltpu.SemaphoreType.DMA((heads + 2 * kv_heads + 3,)),
         pltpu.SemaphoreType.DMA((SEMAPHORES,)),
         pltpu.SemaphoreType.DMA((SEMAPHORES,)),
     ]
@@ -710,7 +729,7 @@
     return pl.pallas_call(
         functools.partial(main_kernel, dims),
         out_shape=jax.ShapeDtypeStruct((CHUNK, tokens), BF16),
-        in_specs=[smem] * 3 + [hbm] * 2 + [vmem] * (len(args) - 5),
+        in_specs=[smem] * 3 + [hbm] * 2 + [vmem] * 6 + [hbm] * 2 + [vmem, hbm, vmem],
         out_specs=vmem,
         scratch_shapes=scratch,
         compiler_params=pltpu.CompilerParams(
@@ -749,8 +768,7 @@
         output_matrix.T,
         output_factor_first[0].T,
         output_factor_second.transpose(1, 2, 0),
-        gate_up_matrix[:, 0, :],
-        gate_up_matrix[:, 1, :],
+        gate_up_matrix,
         gate_up_factor_first[0].T,
         gate_up_factor_second,
         down_matrix,

time: 97.4 us -> 94.5 us (0.970)
  local copies, waits for them, and re-layouts: 3.23 us -> 1.38 us
  Pallas kernels: 94 us -> 92.9 us
    slice x1 -> x0, local copies, waits for them, and re-layouts: 1.21 us -> none  [body(): gate_up_matrix[:, 1, :]]
    pallas_call x1, Pallas kernels: 94 us -> 92.9 us  [main_call(): pl.pallas_call(functools.partial(main_kernel, dims), out_shape=jax.ShapeD...]
where the time goes in v3:
time: 94.5 us; the launch traced here: 94.3 us
  Pallas kernels  92.9 us (98%)
  local copies, waits for them, and re-layouts  1.38 us (1%)
    pallas_call x1, Pallas kernels, main_call(): pl.pallas_call(functools.partial(main_kernel, dims), out_shape=jax.ShapeD...  92.9 us

profile of v3, /device:TPU:16, one launch (start us, length us, event | category | flops | bytes accessed | tf_op | source)
XLA Modules:
  0.0 94.3 jit_solution(1654918815527477539)
XLA Ops:
  0.0 92.9 %shard_map.154 = bf16[32,512]{1,0:T(8,128)(2,1)} custom-call(s32[1,6]{1,0:T(1,128)} %lengths_ref.1, s32[1,6]{1,0:T(1,128)} %adapters_ref.1, s32[64]{0:T(128)} %places_ref.1, bf16[512,2048]{1,0:T(8,128)(2,1)} %queries_ref.1, bf16[512,1024]{1,0:T(8,128)(2,1)} %pairs_ref.1, bf16[32,512]{1,0:T(8,128)(2,1)} %bitcast.19, bf16[1,32]{1,0:T(2,128)(2,1)} %bitcast.21, ...), custom_call_target="tpu_custom_call" | custom-call | tf_op jit(solution)/shard_map/pallas_call | solution.py:729
  92.9 1.4 %copy.18 = bf16[512,32]{0,1:T(8,128)(2,1)} copy(bf16[512,32]{0,1:T(8,128)(2,1)} %bitcast.14) | data formatting | bytes 65536

commit v4 on v3

--- a/solution.py
+++ b/solution.py
@@ -37,14 +37,6 @@
 class Sems:
     def __init__(self, send, recv, used=0):
         self.send, self.recv, self.used = send, recv, used
-
-    def reserve(self, count):
-        part = Sems(self.send, self.recv, self.used)
-        self.used += count
-        return part
-
-    def again(self):
-        return Sems(self.send, self.recv, self.used)
 
     def take(self):
         n = self.used
@@ -92,9 +84,10 @@
     partial,
     pair_in,
     summed,
-    ring_out,
-    ring_in,
-    cross_in,
+    near_in,
+    away_in,
+    on_out,
+    on_in,
     last_out,
     last_in,
     rank_pair,
@@ -155,11 +148,6 @@
             device_id_type=MESH,
         )
 
-    def send(src, dst, pair, device):
-        made = copy(src, dst, pair, device)
-        made.start()
-        return made
-
     def arrived(dst, pair):
         copy(dst, dst, pair, partner()).wait_recv()
 
@@ -198,11 +186,6 @@
     wo_all[z] = wo_ref[...]
     hidden = gate_up_ref.shape[2]
     down_cols = down_ref.shape[1]
-    both = gate_up_ref[...].astype(F32)
-    for n in range(2):
-        gu_all[z, n * hidden : (n + 1) * hidden, :] = both[:, n, :].T.astype(BF16)
-    down_rows = pl.ds(pl.multiple_of(z * down_cols, down_cols), down_cols)
-    down_all[down_rows, :] = down_ref[...].astype(F32).T.astype(BF16)
 
     column = lax.broadcasted_iota(jnp.int32, (1, tokens), 1)
     adapters = bo_ref.shape[2]
@@ -223,83 +206,6 @@
         first = jnp.where(inside, start, first)
         slot_lane = jnp.where(lane // ranks == p, slot, slot_lane)
 
-    pl.semaphore_wait(barrier, len(peers))
-
-    places = [mod(z + k, zs) for k in range(zs)]
-    wo_pairs = [sems.take() for _ in range(zs - 1)]
-    for k in range(1, zs):
-        launch(lambda k=k: copy(wo_all.at[z], wo_all.at[z], wo_pairs[k - 1], to_z(k)))
-    ups, downs = zs // 2, (zs - 1) // 2
-    z_pairs = {}
-    for way, hops in ((1, ups), (-1, downs)):
-        for hop in range(1, hops + 1):
-            z_pairs[way, hop] = (sems.take(), sems.take())
-
-    def z_slot(way, hop):
-        return mod(z - way * hop, zs)
-
-    def z_block(way, hop):
-        slot = z_slot(way, hop)
-        return (
-            gu_all.at[slot],
-            down_all.at[pl.ds(pl.multiple_of(slot * down_cols, down_cols), down_cols), :],
-        )
-
-    def z_wait(hop):
-        for way, hops in ((1, ups), (-1, downs)):
-            if 1 <= hop <= hops:
-                for n, block in enumerate(z_block(way, hop)):
-                    arrived(block, z_pairs[way, hop][n])
-
-    def z_step(hop):
-        z_wait(hop - 1)
-        for way, hops in ((1, ups), (-1, downs)):
-            if hop <= hops:
-                for n in range(2):
-
-                    def make(way=way, n=n):
-                        block = z_block(way, hop - 1)[n]
-                        return copy(block, block, z_pairs[way, hop][n], to_z(way))
-
-                    launch(make)
-
-    factor_y = [None] + [sems.take() for _ in range(1, ys)]
-    factor_x = {(r, k): sems.take() for r in range(ys) for k in range(1, xs)}
-    factor_pair = [sems.take() for _ in range(ys)]
-    near_first = sorted(range(ys), key=lambda k: min(k, ys - k))
-
-    def factor_send():
-        for k in near_first[1:]:
-            launch(lambda k=k: copy(factors.at[c, y, x], factors.at[c, y, x], factor_y[k], to_y(k)))
-
-    def factor_cross():
-        for r in near_first:
-            if r > 0:
-                arrived(factors.at[c, mod(y - r, ys), x], factor_y[r])
-            for k in range(1, xs):
-
-                def make(r=r, k=k):
-                    block = factors.at[c, mod(y - r, ys), x]
-                    return copy(block, block, factor_x[r, k], to_x(k))
-
-                launch(make)
-
-    def factor_share():
-        for r in near_first:
-            for k in range(1, xs):
-                arrived(factors.at[c, mod(y - r, ys), mod(x - k, xs)], factor_x[r, k])
-
-            def make(r=r):
-                block = factors.at[c, mod(y - r, ys)]
-                return copy(block, block, factor_pair[r], partner())
-
-            launch(make)
-
-    def factor_wait():
-        for r in near_first:
-            arrived(factors.at[1 - c, mod(y - r, ys)], factor_pair[r])
-
-    z_step(1)
     adapter_row = lax.broadcasted_iota(jnp.int32, (adapters, 128), 0)
     out_factor = jnp.zeros((CHUNK, 128), F32)
     down_factor = jnp.zeros((CHUNK, 128), F32)
@@ -314,7 +220,112 @@
     gain_lane = prompts * ranks
     out_factor = jnp.where(lane == gain_lane, gain, out_factor)
     factors[c, y, x] = jnp.concatenate([out_factor, down_factor], axis=1).astype(BF16)
-    factor_send()
+
+    pl.semaphore_wait(barrier, len(peers))
+
+    places = [mod(z + k, zs) for k in range(zs)]
+    wo_pairs = [sems.take() for _ in range(zs - 1)]
+    ups, downs = zs // 2, (zs - 1) // 2
+    z_pairs = {}
+    for way, hops in ((1, ups), (-1, downs)):
+        for hop in range(1, hops + 1):
+            z_pairs[way, hop] = (sems.take(), sems.take())
+
+    def z_slot(way, hop):
+        return mod(z - way * hop, zs)
+
+    def z_block(way, hop):
+        slot = z_slot(way, hop)
+        return (
+            gu_all.at[slot],
+            down_all.at[pl.ds(pl.multiple_of(slot * down_cols, down_cols), down_cols), :],
+        )
+
+    def z_wait(hop):
+        for way, hops in ((1, ups), (-1, downs)):
+            if 1 <= hop <= hops:
+                for n, block in enumerate(z_block(way, hop)):
+                    arrived(block, z_pairs[way, hop][n])
+
+    def z_step(hop):
+        z_wait(hop - 1)
+        for way, hops in ((1, ups), (-1, downs)):
+            if hop <= hops:
+                for n in range(2):
+
+                    def make(way=way, n=n):
+                        block = z_block(way, hop - 1)[n]
+                        return copy(block, block, z_pairs[way, hop][n], to_z(way))
+
+                    launch(make)
+
+    near_first = sorted(range(ys), key=lambda k: min(k, ys - k))
+    far_first = near_first[::-1]
+    ways = (1, -1) if xs > 2 else (1,)
+
+    def side(r):
+        return 1 if r % 2 == 0 else -1
+
+    class Gather:
+        def __init__(self, buf):
+            self.buf = buf
+            self.y_pairs = [None] + [sems.take() for _ in range(1, ys)]
+            self.x_pairs = {(r, way): sems.take() for r in range(ys) for way in ways}
+            self.far_pairs = [sems.take() for _ in range(ys)]
+            self.core_pairs = [sems.take() for _ in range(ys)]
+
+        def block(self, r, k):
+            return self.buf.at[c, mod(y - r, ys), mod(x + k, xs)]
+
+        def send(self):
+            for k in near_first[1:]:
+                launch(lambda k=k: copy(self.block(0, 0), self.block(0, 0), self.y_pairs[k], to_y(k)))
+
+        def cross(self, r):
+            if r > 0:
+                arrived(self.block(r, 0), self.y_pairs[r])
+            for way in ways:
+                launch(
+                    lambda way=way: copy(
+                        self.block(r, 0), self.block(r, 0), self.x_pairs[r, way], to_x(way)
+                    )
+                )
+
+        def forward(self, r):
+            for way in ways:
+                arrived(self.block(r, -way), self.x_pairs[r, way])
+            if xs > 2:
+                way = side(r)
+                launch(
+                    lambda: copy(
+                        self.block(r, -way), self.block(r, -way), self.far_pairs[r], to_x(way)
+                    )
+                )
+
+        def share(self, r):
+            if xs > 2:
+                arrived(self.block(r, 2), self.far_pairs[r])
+
+            def make():
+                row = self.buf.at[c, mod(y - r, ys)]
+                return copy(row, row, self.core_pairs[r], partner())
+
+            launch(make)
+
+        def wait(self, r):
+            arrived(self.buf.at[1 - c, mod(y - r, ys)], self.core_pairs[r])
+
+    factor_gather = Gather(factors)
+    middle_gather = Gather(gathered)
+    factor_gather.send()
+    for k in range(1, zs):
+        launch(lambda k=k: copy(wo_all.at[z], wo_all.at[z], wo_pairs[k - 1], to_z(k)))
+    both = gate_up_ref[...].astype(F32)
+    for n in range(2):
+        gu_all[z, n * hidden : (n + 1) * hidden, :] = both[:, n, :].T.astype(BF16)
+    down_rows = pl.ds(pl.multiple_of(z * down_cols, down_cols), down_cols)
+    down_all[down_rows, :] = down_ref[...].astype(F32).T.astype(BF16)
+    z_step(1)
 
     for n in range(2 * kv_heads):
         loads[n].wait()
@@ -351,11 +362,15 @@
             loads[2 * kv_heads + h].wait()
         lax.fori_loop(lo // 2, hi // 2, attend, 0)
 
-    cut = 2 * ((heads * 3) // 8)
-    attend_heads(0, cut)
+    cut_one, cut_two = heads // 2, (3 * heads // 4) // 2 * 2
+    attend_heads(0, cut_one)
+    for r in near_first:
+        factor_gather.cross(r)
+    attend_heads(cut_one, cut_two)
     z_step(2)
-    factor_cross()
-    attend_heads(cut, heads)
+    attend_heads(cut_two, heads)
+    for r in near_first:
+        factor_gather.forward(r)
 
     class AllReduce:
         def __init__(self, pair_buf, x_buf, xin, yin, back):
@@ -420,106 +435,26 @@
     gathered[c, y, x] = base.astype(BF16)
     out_reduce.cross()
 
-    def hops_of(way, j):
-        long = (way == 1) == (j < (xs + 1) // 2)
-        return ys // 2 if long else (ys - 1) // 2
-
-    most = ys // 2
-    ring_keys = [
-        (way, hop, j)
-        for j in range(xs)
-        for way in (1, -1)
-        for hop in range(1, hops_of(way, j) + 1)
-    ]
-    ring_slot = {key: n for n, key in enumerate(ring_keys)}
-    branch_copies = max(xs - 1 + len(ring_keys), ys - 1 + ys * (xs - 1))
-    row_pairs = [sems.take() for _ in range(ys)]
-    gather_sems = sems.reserve(branch_copies)
-
-    def beside_gather():
-        out_reduce.along()
-        factor_share()
-        z_step(3)
-
-    def late_gather():
-        z_step(4)
-
-    def branch(run):
-        kept = len(pending)
-        run()
-        made = pending[kept:]
-        del pending[kept:]
-        return made
-
-    beside = []
-
-    def gather_zero():
-        sems = gather_sems.again()
-        own = gathered.at[0, y, x]
-        x_pairs = [None] + [sems.take() for _ in range(1, xs)]
-        ring = {key: sems.take() for key in ring_keys}
-        sent = []
-        for k in range(1, xs):
-            sent.append(send(own, own, x_pairs[k], to_x(k)))
-        shared = []
-        for hop in range(1, most + 2):
-            for j in range(xs):
-                xj = mod(x - j, xs)
-                if hop == 1 and j > 0:
-                    arrived(gathered.at[0, y, xj], x_pairs[j])
-                for way in (1, -1):
-                    hops = hops_of(way, j)
-                    block = gathered.at[0, mod(y - way * (hop - 1), ys), xj]
-                    if 1 < hop <= hops + 1:
-                        arrived(block, ring[way, hop - 1, j])
-                    if hop <= hops:
-                        sent.append(send(block, block, ring[way, hop, j], to_y(way)))
-            if hop == 1:
-                beside.append(branch(beside_gather))
-            if hop == most:
-                beside.append(branch(late_gather))
-            for k in ((hop - 1) % ys, (1 - hop) % ys):
-                if k not in shared:
-                    shared.append(k)
-                    if k != ys // 2 or hop == most + 1:
-                        block = gathered.at[0, mod(y - k, ys)]
-                        sent.append(send(block, block, row_pairs[k], partner()))
-        for made in sent:
-            made.wait_send()
-
-    def gather_one():
-        sems = gather_sems.again()
-        own = gathered.at[1, y, x]
-        y_pairs = [None] + [sems.take() for _ in range(1, ys)]
-        x_pairs = {(r, k): sems.take() for r in range(ys) for k in range(1, xs)}
-        sent = []
-        for k in near_first[1:]:
-            sent.append(send(own, own, y_pairs[k], to_y(k)))
-        for r in near_first:
-            block = gathered.at[1, mod(y - r, ys), x]
-            if r > 0:
-                arrived(block, y_pairs[r])
-            for k in range(1, xs):
-                sent.append(send(block, block, x_pairs[r, k], to_x(k)))
-            if r == 0:
-                branch(beside_gather)
-        for n, r in enumerate(near_first):
-            if n == ys // 2:
-                branch(late_gather)
-            for k in range(1, xs):
-                arrived(gathered.at[1, mod(y - r, ys), mod(x - k, xs)], x_pairs[r, k])
-            block = gathered.at[1, mod(y - r, ys)]
-            sent.append(send(block, block, row_pairs[r], partner()))
-        for made in sent:
-            made.wait_send()
-
-    pl.when(c == 0)(gather_zero)
-    pl.when(c == 1)(gather_one)
-    pending.extend(beside[0] + beside[1])
-    out_reduce.share()
-    factor_wait()
-    for k in near_first:
-        arrived(gathered.at[1 - c, mod(y - k, ys)], row_pairs[k])
+    middle_gather.send()
+    for n in range(ys + 4):
+        if n < ys:
+            middle_gather.cross(near_first[n])
+        if n == 2:
+            out_reduce.along()
+        if n == 4:
+            z_step(3)
+            for r in near_first:
+                factor_gather.share(r)
+        if 0 <= n - 2 < ys:
+            middle_gather.forward(near_first[n - 2])
+        if 0 <= n - 4 < ys:
+            middle_gather.share(near_first[n - 4])
+        if n == ys:
+            z_step(4)
+            out_reduce.share()
+    for r in near_first:
+        factor_gather.wait(r)
+        middle_gather.wait(r)
 
     out_rank = padded(expand(ADAPTER_SCALE * out_reduce.result()), 128)
     middle_ref[...] += dot(factors[c, y, x, :, :128], out_rank)
@@ -540,7 +475,7 @@
     for load in loads[2 * kv_heads + heads :]:
         load.wait()
     gu_reduce.start(dot(agu_ref[...], normed[...]) * (owned * inverse))
-    for hop in range(5, most + 1):
+    for hop in range(5, ups + 1):
         z_step(hop)
     gu_reduce.cross()
     z_wait(max(ups, downs))
@@ -564,9 +499,9 @@
         [shares[p * ranks : (p + 1) * ranks] * members[p] for p in range(prompts)], axis=0
     ).astype(BF16)
     source = jnp.concatenate([hidden_state, padded(down_rank, 128)], axis=0)
-    far_first = near_first[::-1]
     share_pairs = [sems.take() for _ in range(ys)]
-    scatter_sems = sems.reserve(branch_copies)
+    near_pairs, away_pairs, on_pairs = [[sems.take() for _ in range(ys)] for _ in range(3)]
+    last_pairs = [sems.take() for _ in range(ys)]
     for r in far_first:
         row = mod(y + r, ys)
         weights = down_all[pl.ds(pl.multiple_of(row * per_row, per_row), per_row), :]
@@ -586,88 +521,47 @@
         arrived(pair_in.at[r], share_pairs[r])
         summed[r] = (partial[c, r].astype(F32) + pair_in[r].astype(F32)).astype(BF16)
 
-    def scatter_zero():
-        sems = scatter_sems.again()
-        ring = {key: sems.take() for key in ring_keys}
-        x_pairs = [None] + [sems.take() for _ in range(1, xs)]
-        sent, added = [], []
-        for hop in range(1, most + 1):
-            todo = []
-            for j in range(xs):
-                for way in (1, -1):
-                    hops = hops_of(way, j)
-                    if hop <= hops:
-                        todo.append((j, way, (way * (hops + 1 - hop)) % ys))
-            if hop == 1:
-                todo.sort(key=lambda item: far_first.index(item[2]))
-            for j, way, r in todo:
-                if r not in added:
-                    add_pair(r)
-                    added.append(r)
-                n = ring_slot[way, hop, j]
-                if hop == 1:
-                    block = summed.at[r, j]
-                else:
-                    before = ring_slot[way, hop - 1, j]
-                    arrived(ring_in.at[before], ring[way, hop - 1, j])
-                    total = summed[r, j].astype(F32) + ring_in[before].astype(F32)
-                    ring_out[n] = total.astype(BF16)
-                    block = ring_out.at[n]
-                sent.append(send(block, ring_in.at[n], ring[way, hop, j], to_y(way)))
-            if hop == 1:
-                for r in far_first:
-                    if r not in added:
-                        add_pair(r)
-                        added.append(r)
-        for j in range(xs):
-            total = summed[0, j].astype(F32)
-            for way in (1, -1):
-                hops = hops_of(way, j)
-                if hops > 0:
-                    n = ring_slot[way, hops, j]
-                    arrived(ring_in.at[n], ring[way, hops, j])
-                    total = total + ring_in[n].astype(F32)
-            last_out[j] = total.astype(BF16)
-        for k in range(1, xs):
-            sent.append(send(last_out.at[mod(x + k, xs)], last_in.at[k], x_pairs[k], to_x(k)))
-        total = last_out[x].astype(F32)
-        for k in range(1, xs):
-            arrived(last_in.at[k], x_pairs[k])
-            total = total + last_in[k].astype(F32)
-        middle_ref[...] = middle_ref[...].astype(BF16).astype(F32) + total
-        for made in sent:
-            made.wait_send()
-
-    def scatter_one():
-        sems = scatter_sems.again()
-        x_pairs = {(r, k): sems.take() for r in range(ys) for k in range(1, xs)}
-        y_pairs = [None] + [sems.take() for _ in range(1, ys)]
-        sent = []
-        for r in far_first:
-            add_pair(r)
-            for k in range(1, xs):
-                sent.append(
-                    send(summed.at[r, mod(x + k, xs)], cross_in.at[r, k - 1], x_pairs[r, k], to_x(k))
-                )
-        for r in far_first:
-            total = summed[r, x].astype(F32)
-            for k in range(1, xs):
-                arrived(cross_in.at[r, k - 1], x_pairs[r, k])
-                total = total + cross_in[r, k - 1].astype(F32)
-            last_out[r] = total.astype(BF16)
-            if r > 0:
-                sent.append(send(last_out.at[r], last_in.at[r], y_pairs[r], to_y(r)))
-        total = last_out[0].astype(F32)
-        for r in range(1, ys):
-            arrived(last_in.at[r], y_pairs[r])
-            total = total + last_in[r].astype(F32)
-        middle_ref[...] = middle_ref[...].astype(BF16).astype(F32) + total
-        for made in sent:
-            made.wait_send()
-
-    pl.when(c == 0)(scatter_zero)
-    pl.when(c == 1)(scatter_one)
-    out_ref[...] = middle_ref[...].astype(BF16)
+    def begin(r):
+        add_pair(r)
+        way = side(r) if xs > 2 else 1
+        if xs > 2:
+            launch(
+                lambda: copy(summed.at[r, mod(x + 2, xs)], away_in.at[r], away_pairs[r], to_x(way))
+            )
+        launch(
+            lambda: copy(summed.at[r, mod(x - way, xs)], near_in.at[r], near_pairs[r], to_x(-way))
+        )
+
+    def carry_on(r):
+        if xs > 2:
+            way = side(r)
+            arrived(away_in.at[r], away_pairs[r])
+            total = summed[r, mod(x + way, xs)].astype(F32) + away_in[r].astype(F32)
+            on_out[r] = total.astype(BF16)
+            launch(lambda: copy(on_out.at[r], on_in.at[r], on_pairs[r], to_x(way)))
+
+    def conclude(r):
+        arrived(near_in.at[r], near_pairs[r])
+        total = summed[r, x].astype(F32) + near_in[r].astype(F32)
+        if xs > 2:
+            arrived(on_in.at[r], on_pairs[r])
+            total = total + on_in[r].astype(F32)
+        last_out[r] = total.astype(BF16)
+        if r > 0:
+            launch(lambda: copy(last_out.at[r], last_in.at[r], last_pairs[r], to_y(r)))
+
+    for n in range(ys + 4):
+        if n < ys:
+            begin(far_first[n])
+        if 0 <= n - 2 < ys:
+            carry_on(far_first[n - 2])
+        if 0 <= n - 4 < ys:
+            conclude(far_first[n - 4])
+    total = middle_ref[...].astype(BF16).astype(F32) + last_out[0].astype(F32)
+    for r in near_first[1:]:
+        arrived(last_in.at[r], last_pairs[r])
+        total = total + last_in[r].astype(F32)
+    out_ref[...] = total.astype(BF16)
     for make in pending:
         make().wait_send()
 
@@ -680,7 +574,6 @@
     half = tokens // 2
     span, _, hidden = args[10].shape
     ranks = args[8].shape[0]
-    rings = xs * (ys - 1)
 
     def reduce_buffers(rows, kind):
         return [
@@ -710,12 +603,8 @@
         pltpu.VMEM((CORES, ys, xs, CHUNK, tokens), BF16),
         pltpu.VMEM((ys, xs, CHUNK, tokens), BF16),
         pltpu.VMEM((ys, xs, CHUNK, tokens), BF16),
-        pltpu.VMEM((rings, CHUNK, tokens), BF16),
-        pltpu.VMEM((rings, CHUNK, tokens), BF16),
-        pltpu.VMEM((ys, xs - 1, CHUNK, tokens), BF16),
-        pltpu.VMEM((max(xs, ys), CHUNK, tokens), BF16),
-        pltpu.VMEM((max(xs, ys), CHUNK, tokens), BF16),
     ]
+    scratch += [pltpu.VMEM((ys, CHUNK, tokens), BF16)] * 6
     scratch += reduce_buffers(ranks, BF16)
     scratch += reduce_buffers(2 * ranks, BF16)
     scratch += [

time: 94.5 us -> 88.2 us (0.933)
  the two profiles are of different devices: /device:TPU:16 before, /device:TPU:2 now
where the time goes in v4:
time: 88.2 us; the launch traced here: 88 us
  Pallas kernels  86.6 us (98%)
  local copies, waits for them, and re-layouts  1.38 us (2%)
    pallas_call x1, Pallas kernels, main_call(): pl.pallas_call(functools.partial(main_kernel, dims), out_shape=jax.ShapeD...  86.6 us

profile of v4, /device:TPU:2, one launch (start us, length us, event | category | flops | bytes accessed | tf_op | source)
XLA Modules:
  0.0 88.0 jit_solution(9220098761697456324)
XLA Ops:
  0.0 86.6 %shard_map.154 = bf16[32,512]{1,0:T(8,128)(2,1)} custom-call(s32[1,6]{1,0:T(1,128)} %lengths_ref.1, s32[1,6]{1,0:T(1,128)} %adapters_ref.1, s32[64]{0:T(128)} %places_ref.1, bf16[512,2048]{1,0:T(8,128)(2,1)} %queries_ref.1, bf16[512,1024]{1,0:T(8,128)(2,1)} %pairs_ref.1, bf16[32,512]{1,0:T(8,128)(2,1)} %bitcast.19, bf16[1,32]{1,0:T(2,128)(2,1)} %bitcast.21, ...), custom_call_target="tpu_custom_call" | custom-call | tf_op jit(solution)/shard_map/pallas_call | solution.py:618
  86.6 1.4 %copy.18 = bf16[512,32]{0,1:T(8,128)(2,1)} copy(bf16[512,32]{0,1:T(8,128)(2,1)} %bitcast.14) | data formatting | bytes 65536

commit v5 on v4

--- a/solution.py
+++ b/solution.py
@@ -70,6 +70,7 @@
     bgu_ref,
     ad_ref,
     bias_all,
+    joint_all,
     q_all,
     kv_all,
     values_all,
@@ -353,16 +354,16 @@
             attn_all[pl.ds(pl.multiple_of(h * HEAD, HEAD), HEAD), lo:hi] = (mixed / total).astype(BF16)
 
     def attend(n, carry):
-        attend_one(2 * n)
-        attend_one(2 * n + 1)
+        for k in range(4):
+            attend_one(4 * n + k)
         return carry
 
     def attend_heads(lo, hi):
         for h in range(lo, hi):
             loads[2 * kv_heads + h].wait()
-        lax.fori_loop(lo // 2, hi // 2, attend, 0)
-
-    cut_one, cut_two = heads // 2, (3 * heads // 4) // 2 * 2
+        lax.fori_loop(lo // 4, hi // 4, attend, 0)
+
+    cut_one, cut_two = heads // 2, heads
     attend_heads(0, cut_one)
     for r in near_first:
         factor_gather.cross(r)
@@ -454,21 +455,22 @@
             out_reduce.share()
     for r in near_first:
         factor_gather.wait(r)
-        middle_gather.wait(r)
 
     out_rank = padded(expand(ADAPTER_SCALE * out_reduce.result()), 128)
     middle_ref[...] += dot(factors[c, y, x, :, :128], out_rank)
     per_row = width // ys
     squares = jnp.zeros((8, tokens), F32)
-    for row in range(ys):
+    for r in near_first:
+        middle_gather.wait(r)
+        row = mod(y - r, ys)
         for core in range(CORES):
             block = factors[core, row].reshape(xs * CHUNK, 256)[:, :128]
             full = gathered[core, row].reshape(xs * CHUNK, tokens).astype(F32) + dot(block, out_rank)
             squares = squares + jnp.sum((full * full).reshape(-1, 8, tokens), axis=0)
             scaled = (full * block[:, gain_lane : gain_lane + 1].astype(F32)).astype(BF16)
             for col in range(xs):
-                top = row * per_row + (col * CORES + core) * CHUNK
-                normed[top : top + CHUNK, :] = scaled[col * CHUNK : (col + 1) * CHUNK]
+                top = pl.multiple_of(row * per_row + (col * CORES + core) * CHUNK, CHUNK)
+                normed[pl.ds(top, CHUNK), :] = scaled[col * CHUNK : (col + 1) * CHUNK]
     squares = jnp.sum(squares, axis=0, keepdims=True)
     inverse = lax.rsqrt(squares / width + EPS)
 
@@ -481,19 +483,22 @@
     z_wait(max(ups, downs))
     weights = jnp.concatenate([gu_all[k] for k in range(zs)], axis=1)
     gu_reduce.along()
-    joint = dot(weights, normed[...]) * inverse
+    joint_all[...] = dot(weights, normed[...]) * inverse
+    hidden_factors = []
+    for which in range(2):
+        rows = jnp.concatenate([bgu_ref[which, slot] for slot in slots], axis=0)
+        hidden_factors.append(rows.astype(F32).T.astype(BF16))
+    a_rows = jnp.concatenate([ad_ref[slot] for slot in slots], axis=0)
     gu_reduce.share()
     gu_rank = gu_reduce.result()
 
     def hidden_correction(which, rank):
-        rows = jnp.concatenate([bgu_ref[which, slot] for slot in slots], axis=0)
-        return ADAPTER_SCALE * dot(rows.astype(F32).T.astype(BF16), expand(rank))
-
-    gate = joint[:hidden] + hidden_correction(0, gu_rank[:ranks])
-    up = joint[hidden:] + hidden_correction(1, gu_rank[ranks:])
+        return ADAPTER_SCALE * dot(hidden_factors[which], expand(rank))
+
+    gate = joint_all[:hidden] + hidden_correction(0, gu_rank[:ranks])
+    up = joint_all[hidden:] + hidden_correction(1, gu_rank[ranks:])
     hidden_state = (jax.nn.gelu(gate, approximate=True) * up).astype(BF16)
 
-    a_rows = jnp.concatenate([ad_ref[slot] for slot in slots], axis=0)
     shares = ADAPTER_SCALE * dot(a_rows, hidden_state)
     down_rank = jnp.concatenate(
         [shares[p * ranks : (p + 1) * ranks] * members[p] for p in range(prompts)], axis=0
@@ -589,6 +594,7 @@
         pltpu.VMEM(args[12].shape, BF16),
         pltpu.VMEM(args[14].shape, BF16),
         pltpu.VMEM((tokens, tokens), F32),
+        pltpu.VMEM((2 * hidden, tokens), F32),
         pltpu.VMEM((heads, tokens, HEAD), BF16),
         pltpu.VMEM((2 * kv_heads, tokens, HEAD), BF16),
         pltpu.VMEM((kv_heads, HEAD, tokens), BF16),

time: 88.2 us -> 86.8 us (0.984)
  Pallas kernels: 86.6 us -> 85.2 us
    pallas_call x1, Pallas kernels: 86.6 us -> 85.2 us  [main_call(): pl.pallas_call(functools.partial(main_kernel, dims), out_shape=jax.ShapeD...]
where the time goes in v5:
time: 86.8 us; the launch traced here: 86.6 us
  Pallas kernels  85.2 us (98%)
  local copies, waits for them, and re-layouts  1.38 us (2%)
    pallas_call x1, Pallas kernels, main_call(): pl.pallas_call(functools.partial(main_kernel, dims), out_shape=jax.ShapeD...  85.2 us

profile of v5, /device:TPU:2, one launch (start us, length us, event | category | flops | bytes accessed | tf_op | source)
XLA Modules:
  0.0 86.6 jit_solution(16152781002163319152)
XLA Ops:
  0.0 85.2 %shard_map.154 = bf16[32,512]{1,0:T(8,128)(2,1)} custom-call(s32[1,6]{1,0:T(1,128)} %lengths_ref.1, s32[1,6]{1,0:T(1,128)} %adapters_ref.1, s32[64]{0:T(128)} %places_ref.1, bf16[512,2048]{1,0:T(8,128)(2,1)} %queries_ref.1, bf16[512,1024]{1,0:T(8,128)(2,1)} %pairs_ref.1, bf16[32,512]{1,0:T(8,128)(2,1)} %bitcast.19, bf16[1,32]{1,0:T(2,128)(2,1)} %bitcast.21, ...), custom_call_target="tpu_custom_call" | custom-call | tf_op jit(solution)/shard_map/pallas_call | solution.py:624
  85.2 1.4 %copy.18 = bf16[512,32]{0,1:T(8,128)(2,1)} copy(bf16[512,32]{0,1:T(8,128)(2,1)} %bitcast.14) | data formatting | bytes 65536

commit v6 on v5

--- a/solution.py
+++ b/solution.py
@@ -507,7 +507,40 @@
     share_pairs = [sems.take() for _ in range(ys)]
     near_pairs, away_pairs, on_pairs = [[sems.take() for _ in range(ys)] for _ in range(3)]
     last_pairs = [sems.take() for _ in range(ys)]
-    for r in far_first:
+    def add_pair(r):
+        arrived(pair_in.at[r], share_pairs[r])
+        summed[r] = (partial[c, r].astype(F32) + pair_in[r].astype(F32)).astype(BF16)
+
+    def begin(r):
+        add_pair(r)
+        way = side(r) if xs > 2 else 1
+        if xs > 2:
+            launch(
+                lambda: copy(summed.at[r, mod(x + 2, xs)], away_in.at[r], away_pairs[r], to_x(way))
+            )
+        launch(
+            lambda: copy(summed.at[r, mod(x - way, xs)], near_in.at[r], near_pairs[r], to_x(-way))
+        )
+
+    def carry_on(r):
+        if xs > 2:
+            way = side(r)
+            arrived(away_in.at[r], away_pairs[r])
+            total = summed[r, mod(x + way, xs)].astype(F32) + away_in[r].astype(F32)
+            on_out[r] = total.astype(BF16)
+            launch(lambda: copy(on_out.at[r], on_in.at[r], on_pairs[r], to_x(way)))
+
+    def conclude(r):
+        arrived(near_in.at[r], near_pairs[r])
+        total = summed[r, x].astype(F32) + near_in[r].astype(F32)
+        if xs > 2:
+            arrived(on_in.at[r], on_pairs[r])
+            total = total + on_in[r].astype(F32)
+        last_out[r] = total.astype(BF16)
+        if r > 0:
+            launch(lambda: copy(last_out.at[r], last_in.at[r], last_pairs[r], to_y(r)))
+
+    for n, r in enumerate(far_first):
         row = mod(y + r, ys)
         weights = down_all[pl.ds(pl.multiple_of(row * per_row, per_row), per_row), :]
         extra = jnp.concatenate(
@@ -521,47 +554,20 @@
         launch(
             lambda r=r: copy(partial.at[1 - c, r], pair_in.at[r], share_pairs[r], partner())
         )
-
-    def add_pair(r):
-        arrived(pair_in.at[r], share_pairs[r])
-        summed[r] = (partial[c, r].astype(F32) + pair_in[r].astype(F32)).astype(BF16)
-
-    def begin(r):
-        add_pair(r)
-        way = side(r) if xs > 2 else 1
-        if xs > 2:
-            launch(
-                lambda: copy(summed.at[r, mod(x + 2, xs)], away_in.at[r], away_pairs[r], to_x(way))
-            )
-        launch(
-            lambda: copy(summed.at[r, mod(x - way, xs)], near_in.at[r], near_pairs[r], to_x(-way))
-        )
-
-    def carry_on(r):
-        if xs > 2:
-            way = side(r)
-            arrived(away_in.at[r], away_pairs[r])
-            total = summed[r, mod(x + way, xs)].astype(F32) + away_in[r].astype(F32)
-            on_out[r] = total.astype(BF16)
-            launch(lambda: copy(on_out.at[r], on_in.at[r], on_pairs[r], to_x(way)))
-
-    def conclude(r):
-        arrived(near_in.at[r], near_pairs[r])
-        total = summed[r, x].astype(F32) + near_in[r].astype(F32)
-        if xs > 2:
-            arrived(on_in.at[r], on_pairs[r])
-            total = total + on_in[r].astype(F32)
-        last_out[r] = total.astype(BF16)
-        if r > 0:
-            launch(lambda: copy(last_out.at[r], last_in.at[r], last_pairs[r], to_y(r)))
-
-    for n in range(ys + 4):
-        if n < ys:
+        if n >= 2:
+            begin(far_first[n - 2])
+
+    for n in range(ys - 2, ys + 4):
+        if ys - 2 <= n < ys:
             begin(far_first[n])
-        if 0 <= n - 2 < ys:
+        if n == ys - 2:
+            for before in far_first[: ys - 4]:
+                carry_on(before)
+            for before in far_first[: ys - 6]:
+                conclude(before)
+        if n - 2 < ys:
             carry_on(far_first[n - 2])
-        if 0 <= n - 4 < ys:
-            conclude(far_first[n - 4])
+        conclude(far_first[n - 4])
     total = middle_ref[...].astype(BF16).astype(F32) + last_out[0].astype(F32)
     for r in near_first[1:]:
         arrived(last_in.at[r], last_pairs[r])

time: 86.8 us -> 85.6 us (0.986)
  the two profiles are of different devices: /device:TPU:2 before, /device:TPU:1 now
where the time goes in v6:
time: 85.6 us; the launch traced here: 85.4 us
  Pallas kernels  84 us (98%)
  local copies, waits for them, and re-layouts  1.38 us (2%)
    pallas_call x1, Pallas kernels, main_call(): pl.pallas_call(functools.partial(main_kernel, dims), out_shape=jax.ShapeD...  84 us

profile of v6, /device:TPU:1, one launch (start us, length us, event | category | flops | bytes accessed | tf_op | source)
XLA Modules:
  0.0 85.4 jit_solution(15544371451179569687)
XLA Ops:
  0.0 84.0 %shard_map.154 = bf16[32,512]{1,0:T(8,128)(2,1)} custom-call(s32[1,6]{1,0:T(1,128)} %lengths_ref.1, s32[1,6]{1,0:T(1,128)} %adapters_ref.1, s32[64]{0:T(128)} %places_ref.1, bf16[512,2048]{1,0:T(8,128)(2,1)} %queries_ref.1, bf16[512,1024]{1,0:T(8,128)(2,1)} %pairs_ref.1, bf16[32,512]{1,0:T(8,128)(2,1)} %bitcast.19, bf16[1,32]{1,0:T(2,128)(2,1)} %bitcast.21, ...), custom_call_target="tpu_custom_call" | custom-call | tf_op jit(solution)/shard_map/pallas_call | solution.py:630
  84.0 1.4 %copy.18 = bf16[512,32]{0,1:T(8,128)(2,1)} copy(bf16[512,32]{0,1:T(8,128)(2,1)} %bitcast.14) | data formatting | bytes 65536
